TPU v7x, 256 devices: a whole 4x4x8 slice. The times are simulated.
256 devices in a mesh: plane: 4 (over x), wire: 4 (over z_lo), tick: 16 (over z_hi, y, core).
Axes of the slice: x: 4, y: 4, z: 8 (z_hi: 2, z_lo: 4; z = z_hi * 4 + z_lo), core: 2. Of those that a mesh axis runs over, the one named last changes fastest.
Arguments:
- raw: bfloat16 [4096, 32768], P(('plane', 'wire'), 'tick'), may hold values from -6 to 6
- chan_mask: int32 [4096], P(('plane', 'wire')), may hold values 0 or 1
- kernel: bfloat16 [4, 21, 256], P('plane'), may hold values from -0.078125 to 0.078125
- geometry: bfloat16 [128, 32, 128], replicated, may hold values from -1 to 1
- roi_block: int32 [26112], P(('plane', 'wire', 'tick')), may hold values from 0 to 127, as said below
- roi_owner: int32 [26112], P(('plane', 'wire', 'tick')), may hold values from 0 to 15, as said below
Outputs:
- signal: bfloat16 [4096, 32768], P(('plane', 'wire'), 'tick')
- image: float32 [2048, 32768], P(('plane', 'wire'), 'tick')
Inputs may be any that keep to these rules, and one draw needn't show every extreme that they name: `roi_block`: the 102 ids of one device are distinct. `roi_owner`: owner o is the device of the same tick shard whose index over plane and wire together is o. A device names one owner in at most 25 slots; in every tick shard one owner is named in exactly 25 slots by every device of that shard.
All inputs are finite; a program needn't handle non-finite values. No bound on the sum of `chan_mask` on one device may be relied on, other than what follows from the above.
Results may differ from a plain program's by a relative error of at most 0.0029.
Values may be sent and summed in bfloat16 or wider, within the bound.
A program may use at most 64 MiB of HBM per device.

v0:
```python
import jax
import jax.numpy as jnp
from jax import lax
from jax.sharding import PartitionSpec as P

TB = 128
CAP = 25


def with_halo(array, sides, width):
    for axis, dim in sides:
        devices, length = (lax.axis_size(axis), array.shape[dim])
        up = [(i, (i + 1) % devices) for i in range(devices - 1)]
        down = [(j, i) for i, j in up]
        last = lax.slice_in_dim(array, length - width, length, axis=dim)
        leading = lax.slice_in_dim(array, 0, width, axis=dim)
        before = lax.ppermute(last, axis, up)
        after = lax.ppermute(leading, axis, down)
        array = jnp.concatenate([before, array, after], axis=dim)
    return array


def band_pieces(tap_row, taps_t, band_width):
    row_count = taps_t + band_width
    row_length = taps_t + 2 * band_width
    shifted = jnp.concatenate(
        [
            jnp.zeros((band_width - 1,), tap_row.dtype),
            tap_row,
            jnp.zeros((band_width + 1,), tap_row.dtype),
        ]
    )
    repeated = jnp.tile(shifted, row_count + 1)[: row_count * (row_length + 1)]
    skewed = repeated.reshape(row_count, row_length + 1)[:, :band_width]
    return skewed[::-1]


def deconvolve(padded, kernel_rows, wire_count, tick_count):
    taps_w, taps_t = kernel_rows.shape
    band_width = taps_t // 2
    piece_count = taps_t // band_width + 1
    out_blocks = tick_count // band_width
    in_blocks = (tick_count + taps_t) // band_width

    def add_tap(tap_index, running):
        tap_rows = lax.dynamic_slice_in_dim(padded, tap_index, wire_count, 0)
        tap_rows = tap_rows.reshape(wire_count, in_blocks, band_width)
        tap_row = lax.dynamic_index_in_dim(kernel_rows, tap_index, 0, keepdims=False)
        bands = band_pieces(tap_row, taps_t, band_width)
        for piece in range(piece_count):
            band_now = bands[piece * band_width : (piece + 1) * band_width]
            running = running + jnp.einsum(
                "wjr,rc->wjc",
                tap_rows[:, piece : piece + out_blocks],
                band_now,
                preferred_element_type=jnp.float32,
            )
        return running

    start_sum = jnp.zeros((wire_count, out_blocks, band_width), jnp.float32)
    running = lax.fori_loop(0, taps_w, add_tap, start_sum)
    return running.reshape(wire_count, tick_count).astype(jnp.bfloat16)


def place_slots(owner_list):
    owner_total = lax.axis_size("plane") * lax.axis_size("wire")
    member = (owner_list[:, None] == jnp.arange(owner_total, dtype=jnp.int32)[None, :]).astype(
        jnp.int32
    )
    before = jnp.cumsum(member, axis=0) - member
    return owner_list * CAP + jnp.sum(before * member, axis=1)


def image_from_tiles(geometry, arrived, arrived_tags, tick_blocks):
    geo_index = jnp.maximum(arrived_tags[:, :, 0].astype(jnp.int32), 0)
    tick_index = arrived_tags[:, :, 1].astype(jnp.int32)
    geo_rows = geometry[geo_index]
    cells = geometry.shape[2]

    def add_source(running, source_items):
        geo_now, tiles_now, ticks_now = source_items
        products = jnp.einsum(
            "swc,swt->sct", geo_now, tiles_now, preferred_element_type=jnp.float32
        )
        tick_onehot = (
            ticks_now[:, None] == jnp.arange(tick_blocks, dtype=jnp.int32)[None, :]
        ).astype(jnp.float32)
        running = running + jnp.einsum(
            "sk,sct->ckt", tick_onehot, products, precision=lax.Precision.HIGHEST
        )
        return (running, None)

    start_sum = jnp.zeros((cells, tick_blocks, TB), jnp.float32)
    slice_image, _ = lax.scan(add_source, start_sum, (geo_rows, arrived, tick_index))
    return slice_image


def shards(raw, chan_mask, kernel, geometry, roi_block, roi_owner):
    wire_count, tick_count = raw.shape
    taps_w, taps_t = (kernel.shape[1], kernel.shape[2])
    masked = raw * chan_mask[:, None].astype(jnp.bfloat16)
    padded = with_halo(masked, (("tick", 1),), taps_t // 2)
    padded = with_halo(padded, (("wire", 0),), taps_w // 2)
    signal = deconvolve(padded, kernel[0], wire_count, tick_count)
    block_wires = geometry.shape[1]
    cells = geometry.shape[2]
    wire_blocks = wire_count // block_wires
    tick_blocks = tick_count // TB
    block_tiles = signal.reshape(wire_blocks, block_wires, tick_blocks, TB).transpose(0, 2, 1, 3)
    block_tiles = block_tiles.reshape(wire_blocks * tick_blocks, block_wires, TB)
    chosen = block_tiles[roi_block]
    planes = lax.axis_size("plane")
    wire_shards = lax.axis_size("wire")
    owner_total = planes * wire_shards
    source = lax.axis_index("plane") * wire_shards + lax.axis_index("wire")
    geo_id = source * wire_blocks + roi_block // tick_blocks
    tick_id = roi_block % tick_blocks
    slot_index = place_slots(roi_owner)
    empty_ids = jnp.full((owner_total * CAP,), -1, jnp.int32)
    tick_sent = empty_ids.at[slot_index].set(tick_id)
    payload = (
        jnp.zeros((owner_total * CAP, block_wires, TB), jnp.bfloat16).at[slot_index].set(chosen)
    )
    labels = jnp.stack([empty_ids.at[slot_index].set(geo_id), tick_sent], axis=1).astype(
        jnp.bfloat16
    )
    payload = payload.reshape(owner_total, CAP, block_wires, TB)
    labels = labels.reshape(owner_total, CAP, 2)
    arrived, arrived_tags = (
        lax.all_to_all(payload, ("plane", "wire"), split_axis=0, concat_axis=0, tiled=True),
        lax.all_to_all(labels, ("plane", "wire"), split_axis=0, concat_axis=0, tiled=True),
    )
    slice_image = image_from_tiles(geometry, arrived, arrived_tags, tick_blocks)
    return (signal, slice_image.reshape(cells, tick_count))


def solution(mesh):
    in_specs = (
        P(("plane", "wire"), "tick"),
        P(("plane", "wire")),
        P("plane", None, None),
        P(),
        P(("plane", "wire", "tick")),
        P(("plane", "wire", "tick")),
    )
    out_specs = (P(("plane", "wire"), "tick"), P(("plane", "wire"), "tick"))
    return jax.shard_map(shards, mesh=mesh, in_specs=in_specs, out_specs=out_specs, check_vma=False)
```

profile of v0, /device:TPU:25, one launch (start us, length us, event | category | flops | bytes accessed | tf_op | source)
XLA Modules:
  0.0 488.2 jit_solution(16959877123850198283)
XLA Ops:
  2.8 9.0 %collective-permute-start = (bf16[256,128]{1,0:T(8,128)(2,1)S(1)}, bf16[256,128]{1,0:T(8,128)(2,1)S(1)}, u32[]{:S(2)}, u32[]{:S(2)}) collective-permute-start(bf16[256,128]{1,0:T(8,128)(2,1)S(1)} %get-tuple-element.174), channel_id=1, source_target_pairs={{0,1},{1,2},{2,3},{3,4},{4,5},{5,6},{6,7},{7,8},{8,9},{9,10},{10,1... | collective-permute-start | bytes 196616 | tf_op jit(solution)/shard_map/ppermute | solution.py:17
  16.9 5.5 %all-to-all-start = ((bf16[16,25,2]{1,2,0:T(2,128)(2,1)}), bf16[16,25,2]{1,2,0:T(2,128)(2,1)S(1)}, u32[]{:S(2)}, u32[]{:S(2)}) async-start(bf16[16,25,2]{1,2,0:T(2,128)(2,1)} %copy.34), calls=%async_computation | async-start | bytes 16384 | tf_op jit(solution)/shard_map/all_to_all | solution.py:131
  32.7 262.0 %while.25 = (s32[]{:T(128)}, f32[256,16,128]{2,0,1:T(8,128)}, bf16[276,2304]{1,0:T(8,128)(2,1)}, bf16[21,256]{1,0:T(8,128)(2,1)}, s32[]{:T(128)}, /*index=5*/bf16[]{:T(256)}, s32[]{:T(128)}) while((s32[]{:T(128)}, f32[256,16,128]{2,0,1:T(8,128)}, bf16[276,2304]{1,0:T(8,128)(2,1)}, bf16[21,256]{1,0:T(8,128)(2,1)}, s32[]{:T(128)}, ...), condition=%wide.region_1.2_spmd.clone, body=%wide.region_0.1_spmd.clone.sunk | while | flops 404753408 | bytes 23307364 | solution.py:61
  52.4 4.7 fusion.64
  64.9 4.7 fusion.64
  77.4 4.7 fusion.64
  89.9 4.7 fusion.64
  102.4 4.7 fusion.64
  114.9 4.7 fusion.64
  127.4 4.7 fusion.64
  139.9 4.7 fusion.64
  152.4 4.7 fusion.64
  164.9 4.7 fusion.64
  177.4 4.7 fusion.64
  189.9 4.7 fusion.64
  202.4 4.7 fusion.64
  214.9 4.7 fusion.64
  227.4 4.7 fusion.64
  239.9 4.7 fusion.64
  252.4 4.7 fusion.64
  264.9 4.7 fusion.64
  277.4 4.7 fusion.64
  290.0 4.7 fusion.64
  301.5 12.1 %scatter_fusion = bf16[400,32,128]{2,1,0:T(8,128)(2,1)} fusion(bf16[400,32,128]{2,1,0:T(8,128)(2,1)} %broadcast_in_dim.30, s32[102]{0:T(128)S(1)} %get-tuple-element.179, bf16[102,32,128]{2,1,0:T(8,128)(2,1)S(1)} %copy-done.1), kind=kCustom, calls=%fused_computation.4 | custom fusion | bytes 2507160 | tf_op jit(solution)/shard_map/scatter | solution.py:122
  313.6 5.6 %all-to-all-start.1 = ((bf16[16,25,32,128]{3,2,1,0:T(8,128)(2,1)}), bf16[16,25,32,128]{3,2,1,0:T(8,128)(2,1)}, u32[]{:S(2)}, u32[]{:S(2)}) async-start(bf16[16,25,32,128]{3,2,1,0:T(8,128)(2,1)} %bitcast.76), calls=%async_computation.1 | async-start | bytes 6553600 | tf_op jit(solution)/shard_map/all_to_all | solution.py:130
  323.8 72.9 %all-to-all-done.1 = bf16[16,25,32,128]{3,2,1,0:T(8,128)(2,1)} async-done(((bf16[16,25,32,128]{3,2,1,0:T(8,128)(2,1)}), bf16[16,25,32,128]{3,2,1,0:T(8,128)(2,1)}, u32[]{:S(2)}, u32[]{:S(2)}) %all-to-all-start.1) | async-done | bytes 3276832 | tf_op jit(solution)/shard_map/all_to_all | solution.py:130
  396.7 88.9 %while.26 = (s32[]{:T(128)}, f32[128,16,128]{2,1,0:T(8,128)}, bf16[16,25,32,128]{3,2,1,0:T(8,128)(2,1)}, bf16[16,25,32,128]{3,2,1,0:T(8,128)(2,1)}, s32[16,25]{1,0:T(8,128)S(1)}, /*index=5*/s32[]{:T(128)}, s32[]{:T(128)}) while((s32[]{:T(128)}, f32[128,16,128]{2,1,0:T(8,128)}, bf16[16,25,32,128]{3,2,1,0:T(8,128)(2,1)}, ...), condition=%wide.region_8.9_spmd.clone, body=%wide.region_7.8_spmd.clone.sunk | while | flops 105382288 | bytes 5784967 | solution.py:94
  402.6 4.2 fusion.71
  408.2 4.2 fusion.71
  413.9 4.2 fusion.71
  425.2 4.2 fusion.71
  430.8 4.2 fusion.71
  (406 shorter events, 266.7 us)
Async XLA Ops:
  0.6 318.7 %copy-start = (bf16[128,32,128]{2,1,0:T(8,128)(2,1)S(1)}, bf16[128,32,128]{2,1,0:T(8,128)(2,1)}, u32[]{:S(2)}) copy-start(bf16[128,32,128]{2,1,0:T(8,128)(2,1)} %param.13) | copy-start | bytes 3145732
  0.6 13.2 %copy-start.2 = (s32[102]{0:T(128)S(1)}, s32[102]{0:T(128)}, u32[]{:S(2)}) copy-start(s32[102]{0:T(128)} %param.15) | copy-start | bytes 1228
  0.7 13.6 %copy-start.3 = (s32[102]{0:T(128)S(1)}, s32[102]{0:T(128)}, u32[]{:S(2)}) copy-start(s32[102]{0:T(128)} %param.14) | copy-start | bytes 1228
  2.8 19.6 %collective-permute-start = (bf16[256,128]{1,0:T(8,128)(2,1)S(1)}, bf16[256,128]{1,0:T(8,128)(2,1)S(1)}, u32[]{:S(2)}, u32[]{:S(2)}) collective-permute-start(bf16[256,128]{1,0:T(8,128)(2,1)S(1)} %get-tuple-element.174), channel_id=1, source_target_pairs={{0,1},{1,2},{2,3},{3,4},{4,5},{5,6},{6,7},{7,8},{8,9},{9,10},{10,1... | collective-permute-start | bytes 196616 | tf_op jit(solution)/shard_map/ppermute | solution.py:17
  11.9 11.6 %collective-permute-start.1 = (bf16[256,128]{1,0:T(8,128)(2,1)S(1)}, bf16[256,128]{1,0:T(8,128)(2,1)S(1)}, u32[]{:S(2)}, u32[]{:S(2)}) collective-permute-start(bf16[256,128]{1,0:T(8,128)(2,1)S(1)} %get-tuple-element.175), channel_id=1, source_target_pairs={{1,0},{2,1},{3,2},{4,3},{5,4},{6,5},{7,6},{8,7},{9,8},{10,9},{11,1... | collective-permute-start | bytes 196616 | tf_op jit(solution)/shard_map/ppermute | solution.py:18
  16.9 296.7 %all-to-all-start = ((bf16[16,25,2]{1,2,0:T(2,128)(2,1)}), bf16[16,25,2]{1,2,0:T(2,128)(2,1)S(1)}, u32[]{:S(2)}, u32[]{:S(2)}) async-start(bf16[16,25,2]{1,2,0:T(2,128)(2,1)} %copy.34), calls=%async_computation | async-start | bytes 16384 | tf_op jit(solution)/shard_map/all_to_all | solution.py:131
  23.5 4.1 collective-permute-start.2
  26.2 5.1 %collective-permute-start.3 = (bf16[10,2304]{1,0:T(8,128)(2,1)S(1)}, bf16[10,2304]{1,0:T(8,128)(2,1)S(1)}, u32[]{:S(2)}, u32[]{:S(2)}) collective-permute-start(bf16[10,2304]{1,0:T(8,128)(2,1)S(1)} %get-tuple-element.173), channel_id=1, source_target_pairs={{16,0},{32,16},{48,32},{17,1},{33,17},{49,33},{18,2},{34,18},{50,3... | collective-permute-start | bytes 138248 | tf_op jit(solution)/shard_map/ppermute | solution.py:18
  299.3 2.2 copy-start.1
  313.6 83.1 %all-to-all-start.1 = ((bf16[16,25,32,128]{3,2,1,0:T(8,128)(2,1)}), bf16[16,25,32,128]{3,2,1,0:T(8,128)(2,1)}, u32[]{:S(2)}, u32[]{:S(2)}) async-start(bf16[16,25,32,128]{3,2,1,0:T(8,128)(2,1)} %bitcast.76), calls=%async_computation.1 | async-start | bytes 6553600 | tf_op jit(solution)/shard_map/all_to_all | solution.py:130
where the time goes:
time: 492 us; the launch traced here: 488 us
  matrix products  261 us (53%)
  local copies, waits for them, and re-layouts  115 us (23%)
  waiting for transfers between devices  77.7 us (16%)
  starting transfers between devices  26 us (5%)
  other arithmetic  5.66 us (1%)
    dot_general x63, matrix products, add_tap(): jnp.einsum('wjr,rc->wjc', tap_rows[:, piece:piece + out_blocks], band_now...  173 us
    all_to_all x1, waiting for transfers between devices, shards(): lax.all_to_all(payload, ('plane', 'wire'), split_axis=0, concat_axis=0, t...  72.9 us
    dot_general x16, matrix products, add_source(): jnp.einsum('sk,sct->ckt', tick_onehot, products, precision=lax.Precision....  65.2 us
    dynamic_slice x42, local copies, waits for them, and re-layouts, add_tap(): tap_rows = lax.dynamic_slice_in_dim(padded, tap_index, wire_count, 0)  45.6 us
    dot_general x16, matrix products, add_source(): jnp.einsum('swc,swt->sct', geo_now, tiles_now, preferred_element_type=jnp...  23.2 us
    reshape x21, local copies, waits for them, and re-layouts, band_pieces(): skewed = repeated.reshape(row_count, row_length + 1)[:, :band_width]  17.8 us
    dynamic_slice x21, local copies, waits for them, and re-layouts, add_tap(): lax.dynamic_index_in_dim(kernel_rows, tap_index, 0, keepdims=False)  15 us
    scatter x1, local copies, waits for them, and re-layouts, shards(): jnp.zeros((owner_total * CAP, block_wires, TB), jnp.bfloat16).at[slot_index]  12.1 us
  transfers between devices with their start and end apart: 6, of which 4 were waited for; matrix products, arithmetic and copies ran while one was open for 59% of the time, Pallas kernels for 0%

commit v1 on v0

v1 whole, which is shorter than its diff:
```python
import jax
import jax.numpy as jnp
from jax import lax
from jax.experimental import pallas as pl
from jax.experimental.pallas import tpu as pltpu
from jax.sharding import PartitionSpec as P

TB = 128
VMEM = pl.BlockSpec(memory_space=pltpu.VMEM)
LIMIT = 48 << 20


def with_halo(array, sides, width):
    for axis, dim in sides:
        devices, length = (lax.axis_size(axis), array.shape[dim])
        up = [(i, (i + 1) % devices) for i in range(devices - 1)]
        down = [(j, i) for i, j in up]
        last = lax.slice_in_dim(array, length - width, length, axis=dim)
        leading = lax.slice_in_dim(array, 0, width, axis=dim)
        before = lax.ppermute(last, axis, up)
        after = lax.ppermute(leading, axis, down)
        array = jnp.concatenate([before, array, after], axis=dim)
    return array


def bands_kernel(taps_ref, out_ref):
    row = lax.broadcasted_iota(jnp.int32, (TB, TB), 0)
    col = lax.broadcasted_iota(jnp.int32, (TB, TB), 1)
    upper = col >= row
    zero = jnp.zeros((TB, TB), jnp.float32)
    for a in range(22):
        m, p = a // 2, a % 2
        rolled = [
            pltpu.roll(
                jnp.broadcast_to(taps_ref[a : a + 1, half * TB : (half + 1) * TB], (TB, TB)),
                0,
                1,
                stride=1,
                stride_axis=0,
            )
            for half in range(2)
        ]
        pieces = (
            jnp.where(upper, zero, rolled[1]),
            jnp.where(upper, rolled[1], rolled[0]),
            jnp.where(upper, rolled[0], zero),
        )
        for piece in range(3):
            start = (m * 3 + piece) * TB
            out_ref[start : start + TB, p * TB : (p + 1) * TB] = pieces[piece].astype(jnp.bfloat16)


def make_bands(taps):
    padded = jnp.zeros((24, 2 * TB), jnp.float32).at[: taps.shape[0]].set(taps.astype(jnp.float32))
    return pl.pallas_call(
        bands_kernel,
        out_shape=jax.ShapeDtypeStruct((33 * TB, 2 * TB), jnp.bfloat16),
        in_specs=[VMEM],
        out_specs=VMEM,
        name="bands",
    )(padded)


CHUNK = 64


def deconv_kernel(wave_ref, band_ref, out_ref, tall_ref, shift_ref, sum_ref):
    def spread(i, carry):
        for j in range(18):
            piece = wave_ref[pl.ds(pl.multiple_of(i * 16, 16), 16), j * TB : (j + 1) * TB]
            tall_ref[pl.ds(i * 288 + j, 16, stride=18), :] = piece.astype(jnp.float32)
        return carry

    lax.fori_loop(0, 18, spread, 0)

    def window(i, carry):
        for u in range(8):
            wire = i * 8 + u
            for piece in range(3):
                shift_ref[piece, wire] = tall_ref[pl.ds(wire * 18 + piece, 16), :].astype(jnp.bfloat16)
        return carry

    lax.fori_loop(0, 35, window, 0)

    rows = CHUNK * 16

    def chunk(c, carry):
        first = c * CHUNK
        lhs = jnp.concatenate(
            [
                shift_ref[piece, pl.ds(first + 2 * m, CHUNK + 1)].reshape((CHUNK + 1) * 16, TB)
                for m in range(11)
                for piece in range(3)
            ],
            axis=1,
        )
        both = jnp.dot(lhs, band_ref[...], preferred_element_type=jnp.float32)
        sum_ref[...] = both[:rows, :TB] + both[16:, TB:]
        for j in range(16):
            for b in range(CHUNK // 16):
                start = pl.multiple_of(first + b * 16, 16)
                out_ref[j, pl.ds(start, 16), :] = sum_ref[pl.ds(b * 256 + j, 16, stride=16), :].astype(
                    jnp.bfloat16
                )
        return carry

    lax.fori_loop(0, 256 // CHUNK, chunk, 0)


def deconvolve(padded, bands):
    return pl.pallas_call(
        deconv_kernel,
        out_shape=jax.ShapeDtypeStruct((16, 256, TB), jnp.bfloat16),
        in_specs=[VMEM, VMEM],
        out_specs=VMEM,
        scratch_shapes=[
            pltpu.VMEM((288 * 18, TB), jnp.float32),
            pltpu.VMEM((3, 280, 16, TB), jnp.bfloat16),
            pltpu.VMEM((CHUNK * 16, TB), jnp.float32),
        ],
        compiler_params=pltpu.CompilerParams(vmem_limit_bytes=LIMIT),
        name="deconvolve",
    )(padded, bands)


GROUP = 4


def image_kernel(tiles_ref, geo_ref, owner_ref, out_ref, lhs_ref, total_ref):
    for g in range(16 // GROUP):
        for s in range(GROUP):
            source = g * GROUP + s
            cols = slice(source * 256, (source + 1) * 256)
            owners = owner_ref[source : source + 1, :]
            geo = geo_ref[:, cols]
            for o in range(16):
                keep = jnp.where(owners == o, jnp.float32(1), jnp.float32(0)).astype(jnp.bfloat16)
                lhs_ref[o * TB : (o + 1) * TB, s * 256 : (s + 1) * 256] = geo * keep
        tiles = tiles_ref[g * GROUP : (g + 1) * GROUP].reshape(GROUP * 256, TB)
        part = jnp.dot(lhs_ref[...], tiles, preferred_element_type=jnp.float32)
        if g == 0:
            total_ref[...] = part
        elif g < 16 // GROUP - 1:
            total_ref[...] += part
        else:
            out_ref[...] = (total_ref[...] + part).astype(jnp.bfloat16)


def make_image(tiles, geo, owners):
    return pl.pallas_call(
        image_kernel,
        out_shape=jax.ShapeDtypeStruct((16 * TB, TB), jnp.bfloat16),
        in_specs=[VMEM] * 3,
        out_specs=VMEM,
        scratch_shapes=[
            pltpu.VMEM((16 * TB, GROUP * 256), jnp.bfloat16),
            pltpu.VMEM((16 * TB, TB), jnp.float32),
        ],
        compiler_params=pltpu.CompilerParams(vmem_limit_bytes=LIMIT),
        name="image",
    )(tiles, geo, owners)


def shards(raw, chan_mask, kernel, geometry, roi_block, roi_owner):
    masked = raw * chan_mask[:, None].astype(jnp.bfloat16)
    padded = with_halo(masked, (("tick", 1),), TB)
    padded = with_halo(padded, (("wire", 0),), 10)
    padded = jnp.pad(padded, ((0, 12), (0, 0)))
    tiles = deconvolve(padded, make_bands(kernel[0]))
    signal = tiles.transpose(1, 0, 2).reshape(256, 2048)

    hit = roi_block[:, None] == jnp.arange(128, dtype=jnp.int32)[None, :]
    owner = jnp.sum(jnp.where(hit, roi_owner[:, None] + 1, 0), axis=0) - 1
    owner = jnp.repeat(owner.reshape(8, 16).T, 32, axis=1).astype(jnp.bfloat16)
    group = ("plane", "wire")
    owners = lax.all_to_all(owner, group, split_axis=0, concat_axis=0, tiled=True)
    geo = geometry.reshape(4096, 128).T
    arrived = lax.all_to_all(tiles, group, split_axis=0, concat_axis=0, tiled=True)
    pieces = make_image(arrived, geo, owners.astype(jnp.int32))
    pieces = lax.all_to_all(pieces.reshape(16, TB, TB), group, split_axis=0, concat_axis=0, tiled=True)
    image = pieces.transpose(1, 0, 2).reshape(TB, 2048).astype(jnp.float32)
    return (signal, image)


def solution(mesh):
    in_specs = (
        P(("plane", "wire"), "tick"),
        P(("plane", "wire")),
        P("plane", None, None),
        P(),
        P(("plane", "wire", "tick")),
        P(("plane", "wire", "tick")),
    )
    out_specs = (P(("plane", "wire"), "tick"), P(("plane", "wire"), "tick"))
    return jax.shard_map(shards, mesh=mesh, in_specs=in_specs, out_specs=out_specs, check_vma=False)
```

time: 492 us -> 106 us (0.22)
  matrix products: 261 us -> 0 us
  local copies, waits for them, and re-layouts: 115 us -> 5.64 us
  waiting for transfers between devices: 77.7 us -> 42.2 us
  Pallas kernels: 0 us -> 20.2 us
    dot_general x95 -> x0, matrix products: 261 us -> none  [the longest x63 173 us: add_tap(): jnp.einsum('wjr,rc->wjc', tap_rows[:, piece:piece + out_blocks], band_now...]
    dynamic_slice x63 -> x0, local copies, waits for them, and re-layouts: 60.5 us -> none  [the longest x42 45.6 us: add_tap(): tap_rows = lax.dynamic_slice_in_dim(padded, tap_index, wire_count, 0)]
    all_to_all x2 -> x3, waiting for transfers between devices: 72.9 us -> 39.8 us  [the longest x1 27 us: shards(): lax.all_to_all(tiles, group, split_axis=0, concat_axis=0, tiled=True)]
    pallas_call x0 -> x3, Pallas kernels: none -> 20.2 us  [the longest x1 12.3 us: deconvolve(): pl.pallas_call(deconv_kernel, out_shape=jax.ShapeDtypeStruct((16, 256, TB...]
    reshape x21 -> x1, local copies, waits for them, and re-layouts: 17.8 us -> 0.53 us  [shards(): geo = geometry.reshape(4096, 128).T]
    scatter x3 -> x0, local copies, waits for them, and re-layouts: 13.9 us -> none  [the longest x1 12.1 us: shards(): jnp.zeros((owner_total * CAP, block_wires, TB), jnp.bfloat16).at[slot_index]]
    another operation x87 -> x0, local copies, waits for them, and re-layouts: 6.77 us -> none  [the longest x42 5.84 us: band_pieces(): repeated = jnp.tile(shifted, row_count + 1)[:row_count * (row_length + 1)]]
    all_to_all x2 -> x3, starting transfers between devices: 11.1 us -> 16 us  [the longest x1 6.97 us: shards(): lax.all_to_all(tiles, group, split_axis=0, concat_axis=0, tiled=True)]
  transfers between devices with their start and end apart: 6 -> 7, of which waited for: 4 -> 4; matrix products, arithmetic and copies ran while one was open for 59% -> 6% of each run, Pallas kernels for 0% -> 14%
where the time goes in v1:
time: 106 us; the launch traced here: 105 us
  waiting for transfers between devices  42.2 us (40%)
  starting transfers between devices  30.9 us (29%)
  Pallas kernels  20.2 us (19%)
  local copies, waits for them, and re-layouts  5.64 us (5%)
  other arithmetic  4.9 us (5%)
    all_to_all x1, waiting for transfers between devices, shards(): lax.all_to_all(tiles, group, split_axis=0, concat_axis=0, tiled=True)  27 us
    all_to_all x1, waiting for transfers between devices, shards(): lax.all_to_all(pieces.reshape(16, TB, TB), group, split_axis=0, concat_ax...  12.8 us
    pallas_call x1, Pallas kernels, deconvolve(): pl.pallas_call(deconv_kernel, out_shape=jax.ShapeDtypeStruct((16, 256, TB...  12.3 us
    ppermute x2, starting transfers between devices, with_halo(): before = lax.ppermute(last, axis, up)  11.7 us
    all_to_all x1, starting transfers between devices, shards(): lax.all_to_all(tiles, group, split_axis=0, concat_axis=0, tiled=True)  6.97 us
    all_to_all x1, starting transfers between devices, shards(): lax.all_to_all(owner, group, split_axis=0, concat_axis=0, tiled=True)  5.49 us
    pallas_call x1, Pallas kernels, make_image(): pl.pallas_call(image_kernel, out_shape=jax.ShapeDtypeStruct((16 * TB, TB)...  5.32 us
    all_to_all x1, starting transfers between devices, shards(): lax.all_to_all(pieces.reshape(16, TB, TB), group, split_axis=0, concat_ax...  3.57 us
  transfers between devices with their start and end apart: 7, of which 4 were waited for; matrix products, arithmetic and copies ran while one was open for 6% of the time, Pallas kernels for 14%

profile of v1, /device:TPU:25, one launch (start us, length us, event | category | flops | bytes accessed | tf_op | source)
XLA Modules:
  0.0 104.7 jit_solution(2494944428190991782)
XLA Ops:
  0.7 0.7 convert_element_type.44
  1.3 1.4 %broadcast_multiply_fusion = bf16[256,2048]{1,0:T(8,128)(2,1)S(1)} fusion(bf16[256,2048]{1,0:T(8,128)(2,1)} %param.8, bf16[256]{0:T(256)(128)(2,1)S(1)} %convert_element_type.44), kind=kLoop, calls=%fused_computation.12 | loop fusion | flops 524288 | bytes 2097664 | tf_op jit(solution)/shard_map/mul | solution.py:165
  2.7 0.0 copy-start.2
  2.8 9.0 %collective-permute-start = (bf16[256,128]{1,0:T(8,128)(2,1)S(1)}, bf16[256,128]{1,0:T(8,128)(2,1)S(1)}, u32[]{:S(2)}, u32[]{:S(2)}) collective-permute-start(bf16[256,128]{1,0:T(8,128)(2,1)S(1)} %get-tuple-element.24), channel_id=1, source_target_pairs={{0,1},{1,2},{2,3},{3,4},{4,5},{5,6},{6,7},{7,8},{8,9},{9,10},{10,1... | collective-permute-start | bytes 196616 | tf_op jit(solution)/shard_map/ppermute | solution.py:20
  11.8 1.9 %collective-permute-start.1 = (bf16[256,128]{1,0:T(8,128)(2,1)S(1)}, bf16[256,128]{1,0:T(8,128)(2,1)S(1)}, u32[]{:S(2)}, u32[]{:S(2)}) collective-permute-start(bf16[256,128]{1,0:T(8,128)(2,1)S(1)} %get-tuple-element.25), channel_id=1, source_target_pairs={{1,0},{2,1},{3,2},{4,3},{5,4},{6,5},{7,6},{8,7},{9,8},{10,9},{11,1... | collective-permute-start | bytes 196616 | tf_op jit(solution)/shard_map/ppermute | solution.py:21
  13.8 0.1 select_reduce_fusion
  13.9 0.1 convert_element_type.47
  14.0 0.1 copy.31
  14.0 0.1 broadcast_in_dim.22
  14.1 0.1 convert_element_type.58
  14.2 0.5 broadcast.45
  14.8 0.7 reduce.2
  15.5 0.6 reshape.75
  16.1 5.5 %all-to-all-start.1 = ((bf16[16,2,128]{2,1,0:T(2,128)(2,1)}), bf16[16,2,128]{2,1,0:T(2,128)(2,1)S(1)}, u32[]{:S(2)}, u32[]{:S(2)}) async-start(bf16[16,2,128]{2,1,0:T(2,128)(2,1)} %reshape.75), calls=%async_computation.1 | async-start | bytes 16384 | tf_op jit(solution)/shard_map/all_to_all | solution.py:176
  21.6 1.8 %collective-permute-done.1 = bf16[256,128]{1,0:T(8,128)(2,1)S(1)} collective-permute-done((bf16[256,128]{1,0:T(8,128)(2,1)S(1)}, bf16[256,128]{1,0:T(8,128)(2,1)S(1)}, u32[]{:S(2)}, u32[]{:S(2)}) %collective-permute-start.1) | collective-permute-done | bytes 65568 | tf_op jit(solution)/shard_map/ppermute | solution.py:21
  23.4 2.6 %collective-permute-start.2 = (bf16[10,2304]{1,0:T(8,128)(2,1)S(1)}, bf16[10,2304]{1,0:T(8,128)(2,1)S(1)}, u32[]{:S(2)}, u32[]{:S(2)}) collective-permute-start(bf16[10,2304]{1,0:T(8,128)(2,1)S(1)} %get-tuple-element.22), channel_id=1, source_target_pairs={{0,16},{16,32},{32,48},{1,17},{17,33},{33,49},{2,18},{18,34},{34,5... | collective-permute-start | bytes 138248 | tf_op jit(solution)/shard_map/ppermute | solution.py:20
  26.1 1.3 %collective-permute-start.3 = (bf16[10,2304]{1,0:T(8,128)(2,1)S(1)}, bf16[10,2304]{1,0:T(8,128)(2,1)S(1)}, u32[]{:S(2)}, u32[]{:S(2)}) collective-permute-start(bf16[10,2304]{1,0:T(8,128)(2,1)S(1)} %get-tuple-element.23), channel_id=1, source_target_pairs={{16,0},{32,16},{48,32},{17,1},{33,17},{49,33},{18,2},{34,18},{50,3... | collective-permute-start | bytes 138248 | tf_op jit(solution)/shard_map/ppermute | solution.py:21
  27.4 0.6 pad_convert_fusion.taps_ref
  28.0 2.5 %bands.1.band_ref = bf16[4224,256]{1,0:T(8,128)(2,1)} custom-call(f32[24,256]{1,0:T(8,128)} %pad_convert_fusion.taps_ref), custom_call_target="tpu_custom_call" | custom-call | tf_op jit(solution)/shard_map/bands/pallas_call | solution.py:55
  30.6 0.6 collective-permute-done.3
  31.2 0.3 fusion.6.wave_ref
  31.5 0.7 copy-done
  32.2 12.3 %deconvolve.1 = bf16[16,256,128]{2,1,0:T(8,128)(2,1)} custom-call(bf16[288,2304]{1,0:T(8,128)(2,1)S(1)} %fusion.6.wave_ref, bf16[4224,256]{1,0:T(8,128)(2,1)S(1)} %copy-done), custom_call_target="tpu_custom_call" | custom-call | tf_op jit(solution)/shard_map/deconvolve/pallas_call | solution.py:111
  44.5 7.0 %all-to-all-start = ((bf16[16,256,128]{2,1,0:T(8,128)(2,1)}), bf16[16,256,128]{2,1,0:T(8,128)(2,1)S(1)}, u32[]{:S(2)}, u32[]{:S(2)}) async-start(bf16[16,256,128]{2,1,0:T(8,128)(2,1)} %deconvolve.1), calls=%async_computation | async-start | bytes 2097152 | tf_op jit(solution)/shard_map/all_to_all | solution.py:178
  51.5 0.5 copy.30
  52.0 27.0 %all-to-all-done.tiles_ref = bf16[16,256,128]{2,1,0:T(8,128)(2,1)S(1)} async-done(((bf16[16,256,128]{2,1,0:T(8,128)(2,1)}), bf16[16,256,128]{2,1,0:T(8,128)(2,1)S(1)}, u32[]{:S(2)}, u32[]{:S(2)}) %all-to-all-start) | async-done | bytes 1048608 | tf_op jit(solution)/shard_map/all_to_all | solution.py:178
  79.0 5.3 %image.1 = bf16[2048,128]{1,0:T(8,128)(2,1)} custom-call(bf16[16,256,128]{2,1,0:T(8,128)(2,1)S(1)} %all-to-all-done.tiles_ref, bf16[128,4096]{1,0:T(8,128)(2,1)S(1)} %bitcast.16, s32[16,256]{1,0:T(8,128)S(1)} %bitcast_convert_fusion.owner_ref), custom_call_target="tpu_custom_call" | custom-call | tf_op jit(solution)/shard_map/image/pallas_call | solution.py:150
  84.3 3.6 %all-to-all-start.2 = ((bf16[16,128,128]{2,1,0:T(8,128)(2,1)}), bf16[16,128,128]{2,1,0:T(8,128)(2,1)S(1)}, u32[]{:S(2)}, u32[]{:S(2)}) async-start(bf16[16,128,128]{2,1,0:T(8,128)(2,1)} %bitcast.7), calls=%async_computation.2 | async-start | bytes 1048576 | tf_op jit(solution)/shard_map/all_to_all | solution.py:180
  87.9 1.5 %copy.29 = bf16[256,16,128]{0,2,1:T(8,128)(2,1)S(1)} copy(bf16[256,16,128]{2,0,1:T(8,128)(2,1)} %bitcast.1) | data formatting | bytes 2097152 | tf_op jit(solution)/shard_map/transpose | solution.py:170
  89.4 1.4 %copy.35 = bf16[256,2048]{1,0:T(8,128)(2,1)} copy(bf16[256,2048]{0,1:T(8,128)(2,1)S(1)} %bitcast.17) | data formatting | bytes 2097152
  90.8 12.8 %all-to-all-done.2 = bf16[16,128,128]{2,1,0:T(8,128)(2,1)S(1)} async-done(((bf16[16,128,128]{2,1,0:T(8,128)(2,1)}), bf16[16,128,128]{2,1,0:T(8,128)(2,1)S(1)}, u32[]{:S(2)}, u32[]{:S(2)}) %all-to-all-start.2) | async-done | bytes 524320 | tf_op jit(solution)/shard_map/all_to_all | solution.py:180
  103.6 1.1 %copy_bitcast_fusion = f32[128,2048]{1,0:T(8,128)} fusion(bf16[16,128,128]{2,1,0:T(8,128)(2,1)S(1)} %all-to-all-done.2), kind=kLoop, calls=%fused_computation.10 | loop fusion | flops 262144 | bytes 1572864 | tf_op jit(solution)/shard_map/convert_element_type | solution.py:181
  (17 shorter events, 0.1 us)
Async XLA Ops:
  0.6 13.1 %copy-start.3 = (s32[102]{0:T(128)S(1)}, s32[102]{0:T(128)}, u32[]{:S(2)}) copy-start(s32[102]{0:T(128)} %param.13) | copy-start | bytes 1228
  0.6 13.1 %copy-start.4 = (s32[102]{0:T(128)S(1)}, s32[102]{0:T(128)}, u32[]{:S(2)}) copy-start(s32[102]{0:T(128)} %param.12) | copy-start | bytes 1228
  2.7 24.7 %copy-start.2 = (bf16[1,21,256]{2,1,0:T(8,128)(2,1)S(1)}, bf16[1,21,256]{2,1,0:T(8,128)(2,1)}, u32[]{:S(2)}) copy-start(bf16[1,21,256]{2,1,0:T(8,128)(2,1)} %param.10) | copy-start | bytes 32260
  2.8 18.8 %collective-permute-start = (bf16[256,128]{1,0:T(8,128)(2,1)S(1)}, bf16[256,128]{1,0:T(8,128)(2,1)S(1)}, u32[]{:S(2)}, u32[]{:S(2)}) collective-permute-start(bf16[256,128]{1,0:T(8,128)(2,1)S(1)} %get-tuple-element.24), channel_id=1, source_target_pairs={{0,1},{1,2},{2,3},{3,4},{4,5},{5,6},{6,7},{7,8},{8,9},{9,10},{10,1... | collective-permute-start | bytes 196616 | tf_op jit(solution)/shard_map/ppermute | solution.py:20
  11.8 11.6 %collective-permute-start.1 = (bf16[256,128]{1,0:T(8,128)(2,1)S(1)}, bf16[256,128]{1,0:T(8,128)(2,1)S(1)}, u32[]{:S(2)}, u32[]{:S(2)}) collective-permute-start(bf16[256,128]{1,0:T(8,128)(2,1)S(1)} %get-tuple-element.25), channel_id=1, source_target_pairs={{1,0},{2,1},{3,2},{4,3},{5,4},{6,5},{7,6},{8,7},{9,8},{10,9},{11,1... | collective-permute-start | bytes 196616 | tf_op jit(solution)/shard_map/ppermute | solution.py:21
  16.1 28.4 %all-to-all-start.1 = ((bf16[16,2,128]{2,1,0:T(2,128)(2,1)}), bf16[16,2,128]{2,1,0:T(2,128)(2,1)S(1)}, u32[]{:S(2)}, u32[]{:S(2)}) async-start(bf16[16,2,128]{2,1,0:T(2,128)(2,1)} %reshape.75), calls=%async_computation.1 | async-start | bytes 16384 | tf_op jit(solution)/shard_map/all_to_all | solution.py:176
  23.4 7.1 %collective-permute-start.2 = (bf16[10,2304]{1,0:T(8,128)(2,1)S(1)}, bf16[10,2304]{1,0:T(8,128)(2,1)S(1)}, u32[]{:S(2)}, u32[]{:S(2)}) collective-permute-start(bf16[10,2304]{1,0:T(8,128)(2,1)S(1)} %get-tuple-element.22), channel_id=1, source_target_pairs={{0,16},{16,32},{32,48},{1,17},{17,33},{33,49},{2,18},{18,34},{34,5... | collective-permute-start | bytes 138248 | tf_op jit(solution)/shard_map/ppermute | solution.py:20
  26.1 5.1 %collective-permute-start.3 = (bf16[10,2304]{1,0:T(8,128)(2,1)S(1)}, bf16[10,2304]{1,0:T(8,128)(2,1)S(1)}, u32[]{:S(2)}, u32[]{:S(2)}) collective-permute-start(bf16[10,2304]{1,0:T(8,128)(2,1)S(1)} %get-tuple-element.23), channel_id=1, source_target_pairs={{16,0},{32,16},{48,32},{17,1},{33,17},{49,33},{18,2},{34,18},{50,3... | collective-permute-start | bytes 138248 | tf_op jit(solution)/shard_map/ppermute | solution.py:21
  30.5 1.6 %copy-start = (bf16[4224,256]{1,0:T(8,128)(2,1)S(1)}, bf16[4224,256]{1,0:T(8,128)(2,1)}, u32[]{:S(2)}) copy-start(bf16[4224,256]{1,0:T(8,128)(2,1)} %bands.1.band_ref) | copy-start | bytes 6488068
  44.5 7.0 %copy-start.1 = (bf16[128,32,128]{2,1,0:T(8,128)(2,1)S(1)}, bf16[128,32,128]{2,1,0:T(8,128)(2,1)}, u32[]{:S(2)}) copy-start(bf16[128,32,128]{2,1,0:T(8,128)(2,1)} %param.11) | copy-start | bytes 3145732
  44.5 34.5 %all-to-all-start = ((bf16[16,256,128]{2,1,0:T(8,128)(2,1)}), bf16[16,256,128]{2,1,0:T(8,128)(2,1)S(1)}, u32[]{:S(2)}, u32[]{:S(2)}) async-start(bf16[16,256,128]{2,1,0:T(8,128)(2,1)} %deconvolve.1), calls=%async_computation | async-start | bytes 2097152 | tf_op jit(solution)/shard_map/all_to_all | solution.py:178
  84.3 19.3 %all-to-all-start.2 = ((bf16[16,128,128]{2,1,0:T(8,128)(2,1)}), bf16[16,128,128]{2,1,0:T(8,128)(2,1)S(1)}, u32[]{:S(2)}, u32[]{:S(2)}) async-start(bf16[16,128,128]{2,1,0:T(8,128)(2,1)} %bitcast.7), calls=%async_computation.2 | async-start | bytes 1048576 | tf_op jit(solution)/shard_map/all_to_all | solution.py:180

commit v2 on v1

v2 whole, which is shorter than its diff:
```python
import jax
import jax.numpy as jnp
from jax import lax
from jax.experimental import pallas as pl
from jax.experimental.pallas import tpu as pltpu
from jax.sharding import PartitionSpec as P

TB = 128
N = 16
CHUNK = 64
ROWS = CHUNK * 16
MESH = pl.DeviceIdType.MESH
VMEM = pl.BlockSpec(memory_space=pltpu.VMEM)
ANY = pl.BlockSpec(memory_space=pl.ANY)
BF16 = jnp.bfloat16
F32 = jnp.float32


def row_of(ref, index, size):
    return ref.at[pl.ds(pl.multiple_of(index, size), size)]


def build_bands(taps_ref, band_ref):
    row = lax.broadcasted_iota(jnp.int32, (TB, TB), 0)
    col = lax.broadcasted_iota(jnp.int32, (TB, TB), 1)
    upper = col >= row
    zero = jnp.zeros((TB, TB), F32)

    def pair(m, carry):
        for p in range(2):
            taps = taps_ref[pl.ds(2 * m + p, 1), :]
            low, high = [
                pltpu.roll(
                    jnp.broadcast_to(taps[:, half * TB : (half + 1) * TB], (TB, TB)),
                    0,
                    1,
                    stride=1,
                    stride_axis=0,
                )
                for half in range(2)
            ]
            pieces = (
                jnp.where(upper, zero, high),
                jnp.where(upper, high, low),
                jnp.where(upper, low, zero),
            )
            for piece in range(3):
                start = pl.multiple_of((m * 3 + piece) * TB, TB)
                band_ref[pl.ds(start, TB), p * TB : (p + 1) * TB] = pieces[piece].astype(BF16)
        return carry

    lax.fori_loop(0, 11, pair, 0)


def kernel(
    raw_ref,
    mask_ref,
    taps_ref,
    roi_ref,
    geo_ref,
    signal_ref,
    image_ref,
    edge_t,
    edge_w,
    halo_t,
    halo_w,
    halo_c,
    mask_col,
    tall,
    shifted,
    band,
    sums,
    sig,
    recv,
    own_out,
    own_in,
    geo,
    geo_t,
    masked_geo,
    total,
    piece_out,
    piece_in,
    halo_send,
    halo_recv,
    own_send,
    own_recv,
    tile_send,
    tile_recv,
    image_send,
    image_recv,
    local,
):
    plane, wire, tick = lax.axis_index("plane"), lax.axis_index("wire"), lax.axis_index("tick")
    me = plane * 4 + wire
    up_t, down_t = lax.rem(tick + 1, 16), lax.rem(tick + 15, 16)
    up_w, down_w = lax.rem(wire + 1, 4), lax.rem(wire + 3, 4)

    def member(m):
        return (m // 4, lax.rem(m, 4), tick)

    barrier = pltpu.get_barrier_semaphore()

    def greet(r, carry):
        pl.semaphore_signal(barrier, inc=1, device_id=member(lax.rem(me + r, N)), device_id_type=MESH)
        return carry

    for w in (wire, up_w, down_w):
        for t in (up_t, down_t):
            pl.semaphore_signal(barrier, inc=1, device_id=(plane, w, t), device_id_type=MESH)
    lax.fori_loop(1, N, greet, 0)

    geo_copy = pltpu.make_async_copy(geo_ref, geo, local.at[0])
    geo_copy.start()

    row = lax.broadcasted_iota(jnp.int32, (256, 256), 0)
    col = lax.broadcasted_iota(jnp.int32, (256, 256), 1)
    diag = jnp.where(row == col, mask_ref[...].astype(F32), 0.0).astype(BF16)
    mask_col[...] = jnp.dot(diag, jnp.ones((256, TB), BF16), preferred_element_type=F32)

    ids = roi_ref[0:1, :]
    owner = roi_ref[1:2, :]
    tick_hit = jnp.where(
        lax.broadcasted_iota(jnp.int32, (N, TB), 0) == lax.rem(ids, 16), 1.0, 0.0
    ).astype(BF16)
    wire_hit = jnp.where(
        lax.broadcasted_iota(jnp.int32, (256, TB), 0) // 32 == ids // 16, (owner + 1).astype(F32), 0.0
    ).astype(BF16)
    table = lax.dot_general(tick_hit, wire_hit, (((1,), (1,)), ((), ())), preferred_element_type=F32)
    for m in range(N):
        for half in range(2):
            own_out[m, half : half + 1, :] = table[m : m + 1, half * TB : (half + 1) * TB]
        own_out[m, 2:8, :] = jnp.zeros((6, TB), F32)

    for side, start in ((0, 0), (1, 15 * TB)):
        edge_t[side] = (raw_ref[:, start : start + TB].astype(F32) * mask_col[...]).astype(BF16)
    for side, start in ((0, 0), (1, 240)):
        for j in range(N):
            cols = slice(j * TB, (j + 1) * TB)
            edge_w[side, :, cols] = (
                raw_ref[start : start + 16, cols].astype(F32) * mask_col[start : start + 16, :]
            ).astype(BF16)

    pl.semaphore_wait(barrier, 21)

    first, last = slice(0, TB), slice(15 * TB, 16 * TB)
    halo_copies = [
        pltpu.make_async_remote_copy(
            src_ref=src,
            dst_ref=dst,
            send_sem=halo_send.at[i],
            recv_sem=halo_recv.at[i],
            device_id=(plane, w, t),
            device_id_type=MESH,
        )
        for i, (src, dst, w, t) in enumerate(
            (
                (edge_t.at[1], halo_t.at[0], wire, up_t),
                (edge_t.at[0], halo_t.at[1], wire, down_t),
                (edge_w.at[1], halo_w.at[0], up_w, tick),
                (edge_w.at[0], halo_w.at[1], down_w, tick),
                (edge_w.at[1, :, last], halo_c.at[0], up_w, up_t),
                (edge_w.at[1, :, first], halo_c.at[1], up_w, down_t),
                (edge_w.at[0, :, last], halo_c.at[2], down_w, up_t),
                (edge_w.at[0, :, first], halo_c.at[3], down_w, down_t),
            )
        )
    ]
    for copy in halo_copies:
        copy.start()

    def own_copy(m, source):
        return pltpu.make_async_remote_copy(
            src_ref=own_out.at[m],
            dst_ref=own_in.at[source],
            send_sem=own_send.at[m],
            recv_sem=own_recv.at[source],
            device_id=member(m),
            device_id_type=MESH,
        )

    def send_own(r, carry):
        own_copy(lax.rem(me + r, N), me).start()
        return carry

    lax.fori_loop(1, N, send_own, 0)
    own_in[me] = own_out[me]

    build_bands(taps_ref, band)

    def spread(i, carry):
        wires = pl.ds(pl.multiple_of(i * 16, 16), 16)
        keep = mask_col[wires, :]
        for j in range(N):
            piece = raw_ref[wires, j * TB : (j + 1) * TB].astype(F32) * keep
            tall[pl.ds((i + 1) * 288 + j + 1, 16, stride=18), :] = piece
        return carry

    lax.fori_loop(0, 16, spread, 0)

    tick_ok = [jnp.where(tick == 0, 0.0, 1.0), jnp.where(tick == 15, 0.0, 1.0)]
    wire_ok = [jnp.where(wire == 0, 0.0, 1.0), jnp.where(wire == 3, 0.0, 1.0)]

    def window(i, carry):
        for u in range(8):
            slot = i * 8 + u
            for piece in range(3):
                shifted[piece, slot] = tall[pl.ds(slot * 18 + piece, 16), :].astype(BF16)
        return carry

    for side in range(2):
        halo_copies[side].wait_recv()

    def spread_ticks(i, carry):
        wires = pl.ds(pl.multiple_of(i * 16, 16), 16)
        for side, j in ((0, 0), (1, 17)):
            tall[pl.ds((i + 1) * 288 + j, 16, stride=18), :] = (
                halo_t[side, wires, :].astype(F32) * tick_ok[side]
            )
        return carry

    lax.fori_loop(0, 16, spread_ticks, 0)
    lax.fori_loop(2, 34, window, 0)

    def tile_copy(m, source, part):
        return pltpu.make_async_remote_copy(
            src_ref=sig.at[m, part],
            dst_ref=recv.at[source, part],
            send_sem=tile_send.at[m],
            recv_sem=tile_recv.at[source],
            device_id=member(m),
            device_id_type=MESH,
        )

    def run_chunk(c):
        base = c * CHUNK
        lhs = jnp.concatenate(
            [
                shifted[piece, pl.ds(base + 6 + 2 * m, CHUNK + 1)].reshape((CHUNK + 1) * 16, TB)
                for m in range(11)
                for piece in range(3)
            ],
            axis=1,
        )
        both = jnp.dot(lhs, band[...], preferred_element_type=F32)
        sums[...] = both[:ROWS, :TB] + both[16:, TB:]
        for j in range(N):
            for b in range(CHUNK // 16):
                start = pl.multiple_of(base + b * 16, 16)
                sig[j, pl.ds(start, 16), :] = sums[pl.ds(b * 256 + j, 16, stride=16), :].astype(BF16)
        part = pl.ds(pl.multiple_of(base, CHUNK), CHUNK)

        def send(r, carry):
            tile_copy(lax.rem(me + r, N), me, part).start()
            return carry

        lax.fori_loop(1, N, send, 0)

    def middle(i, carry):
        run_chunk(i + 1)
        return carry

    lax.fori_loop(0, 2, middle, 0)

    for copy in halo_copies[2:]:
        copy.wait_recv()
    for side, base in ((0, 0), (1, 272 * 18)):
        for j in range(N):
            tall[pl.ds(base + j + 1, 16, stride=18), :] = (
                halo_w[side, :, j * TB : (j + 1) * TB].astype(F32) * wire_ok[side]
            )
        for t, j in ((0, 0), (1, 17)):
            tall[pl.ds(base + j, 16, stride=18), :] = (
                halo_c[side * 2 + t].astype(F32) * wire_ok[side] * tick_ok[t]
            )
    lax.fori_loop(0, 2, window, 0)
    lax.fori_loop(34, 36, window, 0)

    def outer(i, carry):
        run_chunk(i * 3)
        return carry

    lax.fori_loop(0, 2, outer, 0)

    def store_signal(j, carry):
        pltpu.make_async_copy(
            sig.at[j], signal_ref.at[:, pl.ds(pl.multiple_of(j * TB, TB), TB)], local.at[1]
        ).start()
        return carry

    lax.fori_loop(0, N, store_signal, 0)
    keep_tile = pltpu.make_async_copy(sig.at[me], recv.at[me], local.at[2])
    keep_tile.start()

    geo_copy.wait()
    row = lax.broadcasted_iota(jnp.int32, (TB, TB), 0)
    col = lax.broadcasted_iota(jnp.int32, (TB, TB), 1)
    eye = jnp.where(row == col, 1.0, 0.0).astype(BF16)

    def turn(s, carry):
        rows = pl.ds(pl.multiple_of(s * 256, 256), 256)
        geo_t[s] = lax.dot_general(
            eye, geo[rows, :], (((1,), (1,)), ((), ())), preferred_element_type=F32
        ).astype(BF16)
        return carry

    lax.fori_loop(0, N, turn, 0)

    def wait_own(r, carry):
        other = lax.rem(me + r, N)
        own_copy(other, other).wait()
        return carry

    lax.fori_loop(1, N, wait_own, 0)

    def source_of(g, i):
        return lax.rem(plane + i, 4) * 4 + lax.rem(wire + g, 4)

    def mask_geo(g, carry):
        for i in range(4):
            s = source_of(g, i)
            for half in range(2):
                owners = own_in[s, half : half + 1, :]
                part = geo_t[s, :, half * TB : (half + 1) * TB]
                for o in range(N):
                    keep = jnp.where(owners == o + 1, 1.0, 0.0).astype(BF16)
                    start = i * 256 + half * TB
                    masked_geo[g, o, :, start : start + TB] = part * keep
        return carry

    lax.fori_loop(0, 4, mask_geo, 0)
    keep_tile.wait()

    def image_copy(o, source):
        return pltpu.make_async_remote_copy(
            src_ref=piece_out.at[o],
            dst_ref=piece_in.at[source],
            send_sem=image_send.at[o],
            recv_sem=image_recv.at[source],
            device_id=member(o),
            device_id_type=MESH,
        )

    everything = pl.ds(0, 256)
    for g in range(4):
        for i in range(4):
            if g or i:
                s = source_of(g, i)
                tile_copy(s, s, everything).wait_recv()
        tiles = jnp.concatenate([recv[source_of(g, i)] for i in range(4)], axis=0)
        for k in range(4):
            members = [lax.rem(me + 1 + 4 * k + i, N) for i in range(4)]
            lhs = jnp.concatenate([masked_geo[g, o] for o in members], axis=0)
            part = jnp.dot(lhs, tiles, preferred_element_type=F32)
            for i, o in enumerate(members):
                now = part[i * TB : (i + 1) * TB]
                if g == 0:
                    total[o] = now
                elif g < 3:
                    total[o] += now
                else:
                    piece_out[o] = (total[o] + now).astype(BF16)
                    if k * 4 + i < N - 1:
                        image_copy(o, me).start()
                    else:
                        piece_in[o] = piece_out[o]

    pltpu.make_async_copy(signal_ref, signal_ref, local.at[1]).wait()
    for copy in halo_copies:
        copy.wait_send()

    def wait_tiles(r, carry):
        tile_copy(lax.rem(me + r, N), me, everything).wait_send()
        return carry

    lax.fori_loop(1, N, wait_tiles, 0)

    def wait_image(r, carry):
        other = lax.rem(me + r, N)
        image_copy(other, other).wait()
        return carry

    lax.fori_loop(1, N, wait_image, 0)
    image_ref[...] = piece_in[...]


def fused(raw, mask, taps, roi, geo):
    dma = pltpu.SemaphoreType.DMA
    return pl.pallas_call(
        kernel,
        out_shape=(
            jax.ShapeDtypeStruct((256, 2048), BF16),
            jax.ShapeDtypeStruct((N, TB, TB), BF16),
        ),
        in_specs=[VMEM, VMEM, VMEM, VMEM, ANY],
        out_specs=(ANY, VMEM),
        scratch_shapes=[
            pltpu.VMEM((2, 256, TB), BF16),
            pltpu.VMEM((2, 16, 2048), BF16),
            pltpu.VMEM((2, 256, TB), BF16),
            pltpu.VMEM((2, 16, 2048), BF16),
            pltpu.VMEM((4, 16, TB), BF16),
            pltpu.VMEM((256, TB), F32),
            pltpu.VMEM((288 * 18, TB), F32),
            pltpu.VMEM((3, 288, 16, TB), BF16),
            pltpu.VMEM((33 * TB, 2 * TB), BF16),
            pltpu.VMEM((ROWS, TB), F32),
            pltpu.VMEM((N, 256, TB), BF16),
            pltpu.VMEM((N, 256, TB), BF16),
            pltpu.VMEM((N, 8, TB), F32),
            pltpu.VMEM((N, 8, TB), F32),
            pltpu.VMEM((4096, TB), BF16),
            pltpu.VMEM((N, TB, 256), BF16),
            pltpu.VMEM((4, N, TB, 1024), BF16),
            pltpu.VMEM((N, TB, TB), F32),
            pltpu.VMEM((N, TB, TB), BF16),
            pltpu.VMEM((N, TB, TB), BF16),
            dma((8,)),
            dma((8,)),
            dma((N,)),
            dma((N,)),
            dma((N,)),
            dma((N,)),
            dma((N,)),
            dma((N,)),
            dma((3,)),
        ],
        compiler_params=pltpu.CompilerParams(
            vmem_limit_bytes=56 << 20, collective_id=0, has_side_effects=True
        ),
        name="fused",
    )(raw, mask, taps, roi, geo)


def shards(raw, chan_mask, kernel_rows, geometry, roi_block, roi_owner):
    taps = jnp.zeros((24, 2 * TB), F32).at[:21].set(kernel_rows[0].astype(F32))
    slots = roi_block.shape[0]
    roi = jnp.full((2, TB), -1, jnp.int32).at[:, :slots].set(jnp.stack([roi_block, roi_owner]))
    signal, pieces = fused(raw, chan_mask.reshape(1, 256), taps, roi, geometry.reshape(4096, TB))
    image = pieces.transpose(1, 0, 2).reshape(TB, 2048).astype(F32)
    return (signal, image)


def solution(mesh):
    in_specs = (
        P(("plane", "wire"), "tick"),
        P(("plane", "wire")),
        P("plane", None, None),
        P(),
        P(("plane", "wire", "tick")),
        P(("plane", "wire", "tick")),
    )
    out_specs = (P(("plane", "wire"), "tick"), P(("plane", "wire"), "tick"))
    return jax.shard_map(shards, mesh=mesh, in_specs=in_specs, out_specs=out_specs, check_vma=False)
```

time: 106 us -> 62.3 us (0.59)
  the two profiles are of different devices: /device:TPU:25 before, /device:TPU:64 now
where the time goes in v2:
time: 62.3 us; the launch traced here: 62.1 us
  Pallas kernels  54.6 us (88%)
  other arithmetic  3.71 us (6%)
  local copies, waits for them, and re-layouts  3.18 us (5%)
  between operations  0.67 us (1%)
    pallas_call x1, Pallas kernels, fused(): pl.pallas_call(kernel, out_shape=(jax.ShapeDtypeStruct((256, 2048), BF16)...  54.6 us
    unnamed x6, local copies, waits for them, and re-layouts  2.29 us
    another operation x2, other arithmetic  1.97 us

profile of v2, /device:TPU:64, one launch (start us, length us, event | category | flops | bytes accessed | tf_op | source)
XLA Modules:
  0.0 62.1 jit_solution(11863462474539961473)
XLA Ops:
  0.6 0.0 copy-start.1
  0.6 0.6 %compare_reduce_fusion = pred[]{:T(512)} fusion(), kind=kLoop, calls=%fused_computation.2 | loop fusion | flops 5 | bytes 1 | tf_op jit(solution)/shard_map/reduce.3
  1.3 1.3 %add_select_fusion = s32[2,102]{1,0:T(2,128)S(1)} fusion(s32[1,102]{1,0:T(1,128)} %bitcast.12, s32[1,102]{1,0:T(1,128)} %bitcast.13, pred[]{:T(512)} %compare_reduce_fusion), kind=kLoop, calls=%fused_computation.3 | loop fusion | flops 408 | bytes 1633 | tf_op jit(solution)/shard_map/select.3
  2.6 0.6 scatter.14.roi_ref
  3.2 0.0 copy-done.1
  3.2 0.6 pad_convert_fusion.taps_ref
  3.8 54.6 %fused.1 = (bf16[256,2048]{1,0:T(8,128)(2,1)}, bf16[16,128,128]{2,1,0:T(8,128)(2,1)}) custom-call(bf16[256,2048]{1,0:T(8,128)(2,1)} %raw_ref.1, s32[1,256]{1,0:T(1,128)} %bitcast.11, f32[24,256]{1,0:T(8,128)} %pad_convert_fusion.taps_ref, s32[2,128]{1,0:T(2,128)} %scatter.14.roi_ref, bf16[4096,128]{1,0:T(8,128)(2,1)} %bitcast.9), custom_call_target="tpu_custom_call" | custom-call | tf_op jit(solution)/shard_map/fused/pallas_call | solution.py:388
  58.4 1.1 %convert_bitcast_fusion = f32[128,16,128]{2,0,1:T(8,128)S(1)} fusion(bf16[16,128,128]{2,1,0:T(8,128)(2,1)} %get-tuple-element.29), kind=kLoop, calls=%fused_computation | loop fusion | flops 262144 | bytes 1572864 | tf_op jit(solution)/shard_map/convert_element_type | solution.py:439
  59.5 0.3 copy.8
  59.8 0.0 copy-start
  59.8 1.3 %copy.9 = f32[128,2048]{1,0:T(8,128)} copy(f32[128,2048]{0,1:T(8,128)S(1)} %bitcast.8) | data formatting | bytes 2097152
  61.2 0.0 copy-done
  61.2 1.0 %copy.11 = bf16[256,2048]{1,0:T(8,128)(2,1)} copy(bf16[256,2048]{1,0:T(8,128)(2,1)S(1)} %copy-done) | data formatting | bytes 2097152
Async XLA Ops:
  0.6 2.5 %copy-start.1 = (bf16[1,21,256]{2,1,0:T(8,128)(2,1)S(1)}, bf16[1,21,256]{2,1,0:T(8,128)(2,1)}, u32[]{:S(2)}) copy-start(bf16[1,21,256]{2,1,0:T(8,128)(2,1)} %param.12) | copy-start | bytes 32260
  59.8 1.3 %copy-start = (bf16[256,2048]{1,0:T(8,128)(2,1)S(1)}, bf16[256,2048]{1,0:T(8,128)(2,1)}, u32[]{:S(2)}) copy-start(bf16[256,2048]{1,0:T(8,128)(2,1)} %get-tuple-element.34) | copy-start | bytes 3145732

commit v3 on v2

--- a/solution.py
+++ b/solution.py
@@ -53,13 +53,17 @@
 
 
 def kernel(
-    raw_ref,
+    raw_hbm,
     mask_ref,
     taps_ref,
-    roi_ref,
+    block_ref,
+    owner_ref,
     geo_ref,
     signal_ref,
     image_ref,
+    raw_ref,
+    taps,
+    roi_ref,
     edge_t,
     edge_w,
     halo_t,
@@ -92,6 +96,11 @@
 ):
     plane, wire, tick = lax.axis_index("plane"), lax.axis_index("wire"), lax.axis_index("tick")
     me = plane * 4 + wire
+    half, inner = wire // 2, lax.rem(wire, 2)
+    spot = plane * 2 + inner
+    whole = jnp.logical_or(wire == 1, wire == 2)
+    split = jnp.logical_not(whole)
+    mine = plane * 2 + half
     up_t, down_t = lax.rem(tick + 1, 16), lax.rem(tick + 15, 16)
     up_w, down_w = lax.rem(wire + 1, 4), lax.rem(wire + 3, 4)
 
@@ -109,8 +118,15 @@
             pl.semaphore_signal(barrier, inc=1, device_id=(plane, w, t), device_id_type=MESH)
     lax.fori_loop(1, N, greet, 0)
 
+    raw_copy = pltpu.make_async_copy(raw_hbm, raw_ref, local.at[3])
+    raw_copy.start()
     geo_copy = pltpu.make_async_copy(geo_ref, geo, local.at[0])
     geo_copy.start()
+    taps[...] = jnp.zeros((24, 2 * TB), F32)
+    taps[0:21, :] = taps_ref[...].astype(F32)
+    roi_ref[...] = jnp.full((8, TB), -1, jnp.int32)
+    roi_ref[0:1, 0:102] = block_ref[...]
+    roi_ref[1:2, 0:102] = owner_ref[...]
 
     row = lax.broadcasted_iota(jnp.int32, (256, 256), 0)
     col = lax.broadcasted_iota(jnp.int32, (256, 256), 1)
@@ -127,10 +143,11 @@
     ).astype(BF16)
     table = lax.dot_general(tick_hit, wire_hit, (((1,), (1,)), ((), ())), preferred_element_type=F32)
     for m in range(N):
-        for half in range(2):
-            own_out[m, half : half + 1, :] = table[m : m + 1, half * TB : (half + 1) * TB]
+        for side in range(2):
+            own_out[m, side : side + 1, :] = table[m : m + 1, side * TB : (side + 1) * TB]
         own_out[m, 2:8, :] = jnp.zeros((6, TB), F32)
 
+    raw_copy.wait()
     for side, start in ((0, 0), (1, 15 * TB)):
         edge_t[side] = (raw_ref[:, start : start + TB].astype(F32) * mask_col[...]).astype(BF16)
     for side, start in ((0, 0), (1, 240)):
@@ -168,24 +185,89 @@
     for copy in halo_copies:
         copy.start()
 
-    def own_copy(m, source):
+    def to_whole(a, src, dst, send, receive):
         return pltpu.make_async_remote_copy(
-            src_ref=own_out.at[m],
-            dst_ref=own_in.at[source],
-            send_sem=own_send.at[m],
-            recv_sem=own_recv.at[source],
-            device_id=member(m),
+            src_ref=src(a),
+            dst_ref=dst(half, spot),
+            send_sem=send.at[a],
+            recv_sem=receive.at[half, spot],
+            device_id=(a // 2, 1 + lax.rem(a, 2), tick),
             device_id_type=MESH,
         )
 
-    def send_own(r, carry):
-        own_copy(lax.rem(me + r, N), me).start()
-        return carry
-
-    lax.fori_loop(1, N, send_own, 0)
-    own_in[me] = own_out[me]
-
-    build_bands(taps_ref, band)
+    def to_split(p, h, src, dst, send, receive):
+        return pltpu.make_async_remote_copy(
+            src_ref=src(8 + 2 * p + h),
+            dst_ref=dst(h, spot),
+            send_sem=send.at[8 + 2 * p + h],
+            recv_sem=receive.at[h, spot],
+            device_id=(p, 3 * half, tick),
+            device_id_type=MESH,
+        )
+
+    def exchange(act, *refs):
+        def wholes(r, carry):
+            act(to_whole(lax.rem(mine + r, 8), *refs))
+            return carry
+
+        def splits(r, carry):
+            for h in range(2):
+                act(to_split(lax.rem(plane + r, 4), h, *refs))
+            return carry
+
+        lax.fori_loop(1, 8, wholes, 0)
+        lax.fori_loop(1, 4, splits, 0)
+
+        @pl.when(split)
+        def _():
+            act(to_whole(mine, *refs))
+
+        @pl.when(whole)
+        def _():
+            for h in range(2):
+                act(to_split(plane, h, *refs))
+
+    def begin(copy):
+        copy.start()
+
+    def wait_send(copy):
+        copy.wait_send()
+
+    def arrival(h, other, dst, receive):
+        return pltpu.make_async_remote_copy(
+            src_ref=dst(h, other),
+            dst_ref=dst(h, other),
+            send_sem=receive.at[h, other],
+            recv_sem=receive.at[h, other],
+            device_id=(other // 2, 2 * jnp.where(whole, h, half) + lax.rem(other, 2), tick),
+            device_id_type=MESH,
+        )
+
+    def wait_half(h, second, dst, receive):
+        def one(r, carry):
+            arrival(h, lax.rem(spot + r, 8), dst, receive).wait_recv()
+            return carry
+
+        lax.fori_loop(1, 8, one, 0)
+        if second:
+
+            @pl.when(whole)
+            def _():
+                arrival(h, spot, dst, receive).wait_recv()
+
+    own_refs = (lambda j: own_out.at[j], lambda h, i: own_in.at[h, i], own_send, own_recv)
+    exchange(begin, *own_refs)
+
+    @pl.when(whole)
+    def _():
+        own_in[half, spot] = own_out[mine]
+
+    @pl.when(split)
+    def _():
+        for h in range(2):
+            own_in[h, spot] = own_out[8 + 2 * plane + h]
+
+    build_bands(taps, band)
 
     def spread(i, carry):
         wires = pl.ds(pl.multiple_of(i * 16, 16), 16)
@@ -197,6 +279,20 @@
 
     lax.fori_loop(0, 16, spread, 0)
 
+    geo_copy.wait()
+    row = lax.broadcasted_iota(jnp.int32, (TB, TB), 0)
+    col = lax.broadcasted_iota(jnp.int32, (TB, TB), 1)
+    eye = jnp.where(row == col, 1.0, 0.0).astype(BF16)
+
+    def turn(s, carry):
+        rows = pl.ds(pl.multiple_of(s * 256, 256), 256)
+        geo_t[s] = lax.dot_general(
+            eye, geo[rows, :], (((1,), (1,)), ((), ())), preferred_element_type=F32
+        ).astype(BF16)
+        return carry
+
+    lax.fori_loop(0, N, turn, 0)
+
     tick_ok = [jnp.where(tick == 0, 0.0, 1.0), jnp.where(tick == 15, 0.0, 1.0)]
     wire_ok = [jnp.where(wire == 0, 0.0, 1.0), jnp.where(wire == 3, 0.0, 1.0)]
 
@@ -220,16 +316,6 @@
 
     lax.fori_loop(0, 16, spread_ticks, 0)
     lax.fori_loop(2, 34, window, 0)
-
-    def tile_copy(m, source, part):
-        return pltpu.make_async_remote_copy(
-            src_ref=sig.at[m, part],
-            dst_ref=recv.at[source, part],
-            send_sem=tile_send.at[m],
-            recv_sem=tile_recv.at[source],
-            device_id=member(m),
-            device_id_type=MESH,
-        )
 
     def run_chunk(c):
         base = c * CHUNK
@@ -249,11 +335,7 @@
                 sig[j, pl.ds(start, 16), :] = sums[pl.ds(b * 256 + j, 16, stride=16), :].astype(BF16)
         part = pl.ds(pl.multiple_of(base, CHUNK), CHUNK)
 
-        def send(r, carry):
-            tile_copy(lax.rem(me + r, N), me, part).start()
-            return carry
-
-        lax.fori_loop(1, N, send, 0)
+        exchange(begin, lambda j: sig.at[j, part], lambda h, i: recv.at[h, i, part], tile_send, tile_recv)
 
     def middle(i, carry):
         run_chunk(i + 1)
@@ -288,112 +370,182 @@
         return carry
 
     lax.fori_loop(0, N, store_signal, 0)
-    keep_tile = pltpu.make_async_copy(sig.at[me], recv.at[me], local.at[2])
-    keep_tile.start()
-
-    geo_copy.wait()
-    row = lax.broadcasted_iota(jnp.int32, (TB, TB), 0)
-    col = lax.broadcasted_iota(jnp.int32, (TB, TB), 1)
-    eye = jnp.where(row == col, 1.0, 0.0).astype(BF16)
-
-    def turn(s, carry):
-        rows = pl.ds(pl.multiple_of(s * 256, 256), 256)
-        geo_t[s] = lax.dot_general(
-            eye, geo[rows, :], (((1,), (1,)), ((), ())), preferred_element_type=F32
-        ).astype(BF16)
-        return carry
-
-    lax.fori_loop(0, N, turn, 0)
-
-    def wait_own(r, carry):
-        other = lax.rem(me + r, N)
-        own_copy(other, other).wait()
-        return carry
-
-    lax.fori_loop(1, N, wait_own, 0)
-
-    def source_of(g, i):
-        return lax.rem(plane + i, 4) * 4 + lax.rem(wire + g, 4)
-
-    def mask_geo(g, carry):
-        for i in range(4):
-            s = source_of(g, i)
-            for half in range(2):
-                owners = own_in[s, half : half + 1, :]
-                part = geo_t[s, :, half * TB : (half + 1) * TB]
+
+    @pl.when(whole)
+    def _():
+        recv[half, spot] = sig[mine]
+
+    @pl.when(split)
+    def _():
+        for h in range(2):
+            recv[h, spot] = sig[8 + 2 * plane + h]
+
+    first_half = jnp.where(whole, half, 0)
+    own_dst, tile_dst = own_refs[1], lambda h, i: recv.at[h, i]
+    wait_half(first_half, False, own_dst, own_recv)
+    wait_half(1 - first_half, True, own_dst, own_recv)
+
+    def mask_geo(i, carry):
+        for h in range(2):
+            wires = jnp.where(whole, h, half)
+            s = (i // 2) * 4 + 2 * wires + lax.rem(i, 2)
+            for side in range(2):
+                owners = own_in[h, i, side : side + 1, :]
+                part = geo_t[s, :, side * TB : (side + 1) * TB]
+                cols = pl.ds(pl.multiple_of(i * 256 + side * TB, TB), TB)
                 for o in range(N):
                     keep = jnp.where(owners == o + 1, 1.0, 0.0).astype(BF16)
-                    start = i * 256 + half * TB
-                    masked_geo[g, o, :, start : start + TB] = part * keep
-        return carry
-
-    lax.fori_loop(0, 4, mask_geo, 0)
-    keep_tile.wait()
-
-    def image_copy(o, source):
+                    masked_geo[h, o, :, cols] = part * keep
+        return carry
+
+    lax.fori_loop(0, 8, mask_geo, 0)
+
+    def image_slot(p, w, h, k):
+        outer = jnp.logical_or(w == 0, w == 3)
+        return jnp.where(outer, 8 + (2 * p + k) * 2 + h, 2 * p + h)
+
+    def image_copy(k, o):
+        slot = image_slot(plane, wire, half, k)
         return pltpu.make_async_remote_copy(
-            src_ref=piece_out.at[o],
-            dst_ref=piece_in.at[source],
-            send_sem=image_send.at[o],
-            recv_sem=image_recv.at[source],
+            src_ref=piece_out.at[k, o],
+            dst_ref=piece_in.at[slot],
+            send_sem=image_send.at[k, o],
+            recv_sem=image_recv.at[slot],
             device_id=member(o),
             device_id_type=MESH,
         )
 
-    everything = pl.ds(0, 256)
-    for g in range(4):
-        for i in range(4):
-            if g or i:
-                s = source_of(g, i)
-                tile_copy(s, s, everything).wait_recv()
-        tiles = jnp.concatenate([recv[source_of(g, i)] for i in range(4)], axis=0)
-        for k in range(4):
-            members = [lax.rem(me + 1 + 4 * k + i, N) for i in range(4)]
-            lhs = jnp.concatenate([masked_geo[g, o] for o in members], axis=0)
+    both_halves = jnp.where(whole, 1.0, 0.0)
+    for turn_now in range(2):
+        h = first_half if turn_now == 0 else 1 - first_half
+        k = 0 if turn_now == 0 else jnp.where(whole, 0, 1)
+        wait_half(h, turn_now == 1, tile_dst, tile_recv)
+        tiles = recv[h].reshape(2048, TB)
+        for quarter in range(4):
+            members = [lax.rem(me + 1 + 4 * quarter + i, N) for i in range(4)]
+            lhs = jnp.concatenate([masked_geo[h, o] for o in members], axis=0)
             part = jnp.dot(lhs, tiles, preferred_element_type=F32)
             for i, o in enumerate(members):
                 now = part[i * TB : (i + 1) * TB]
-                if g == 0:
+                if turn_now == 0:
                     total[o] = now
-                elif g < 3:
-                    total[o] += now
                 else:
-                    piece_out[o] = (total[o] + now).astype(BF16)
-                    if k * 4 + i < N - 1:
-                        image_copy(o, me).start()
+                    now = now + total[o] * both_halves
+
+                def send_piece():
+                    piece_out[k, o] = now.astype(BF16)
+                    if quarter * 4 + i < N - 1:
+                        image_copy(k, o).start()
                     else:
-                        piece_in[o] = piece_out[o]
-
-    pltpu.make_async_copy(signal_ref, signal_ref, local.at[1]).wait()
+                        piece_in[image_slot(plane, wire, half, k)] = piece_out[k, o]
+
+                if turn_now == 0:
+                    pl.when(split)(send_piece)
+                else:
+                    send_piece()
+
     for copy in halo_copies:
         copy.wait_send()
-
-    def wait_tiles(r, carry):
-        tile_copy(lax.rem(me + r, N), me, everything).wait_send()
-        return carry
-
-    lax.fori_loop(1, N, wait_tiles, 0)
-
-    def wait_image(r, carry):
-        other = lax.rem(me + r, N)
-        image_copy(other, other).wait()
-        return carry
-
-    lax.fori_loop(1, N, wait_image, 0)
+    exchange(wait_send, *own_refs)
+    exchange(wait_send, lambda j: sig.at[j], tile_dst, tile_send, tile_recv)
+    pltpu.make_async_copy(signal_ref, signal_ref, local.at[1]).wait()
+
+    def wait_image_send(k):
+        def one(r, carry):
+            image_copy(k, lax.rem(me + r, N)).wait_send()
+            return carry
+
+        lax.fori_loop(1, N, one, 0)
+
+    wait_image_send(0)
+
+    @pl.when(split)
+    def _():
+        wait_image_send(1)
+
+    def image_arrival(slot):
+        return pltpu.make_async_remote_copy(
+            src_ref=piece_in.at[slot],
+            dst_ref=piece_in.at[slot],
+            send_sem=image_recv.at[slot],
+            recv_sem=image_recv.at[slot],
+            device_id=(plane, up_w, tick),
+            device_id_type=MESH,
+        )
+
+    def whole_images(r, carry):
+        image_arrival(lax.rem(mine + r, 8)).wait_recv()
+        return carry
+
+    def split_images(r, carry):
+        for k in range(2):
+            for h in range(2):
+                image_arrival(8 + (2 * lax.rem(plane + r, 4) + k) * 2 + h).wait_recv()
+        return carry
+
+    lax.fori_loop(1, 8, whole_images, 0)
+    lax.fori_loop(1, 4, split_images, 0)
+    for k in range(2):
+        image_arrival(8 + (2 * plane + k) * 2 + 1 - half).wait_recv()
+
+    @pl.when(split)
+    def _():
+        image_arrival(mine).wait_recv()
+
+    @pl.when(whole)
+    def _():
+        for k in range(2):
+            image_arrival(8 + (2 * plane + k) * 2 + half).wait_recv()
+
     image_ref[...] = piece_in[...]
 
 
-def fused(raw, mask, taps, roi, geo):
+def finish_kernel(signal_ref, piece_ref, signal_out, image_ref, held, sem):
+    parts = [pl.ds(i * 64, 64) for i in range(4)]
+    loads = [pltpu.make_async_copy(signal_ref.at[p], held.at[p], sem.at[0, i]) for i, p in enumerate(parts)]
+    stores = [pltpu.make_async_copy(held.at[p], signal_out.at[p], sem.at[1, i]) for i, p in enumerate(parts)]
+    for load in loads:
+        load.start()
+    for load, store in zip(loads, stores):
+        load.wait()
+        store.start()
+    for j in range(8):
+        image_ref[:, j * TB : (j + 1) * TB] = piece_ref[j].astype(F32)
+        image_ref[:, (8 + j) * TB : (9 + j) * TB] = piece_ref[8 + 2 * j].astype(F32) + piece_ref[
+            9 + 2 * j
+        ].astype(F32)
+    for store in stores:
+        store.wait()
+
+
+def finish(signal, pieces):
+    return pl.pallas_call(
+        finish_kernel,
+        out_shape=(
+            jax.ShapeDtypeStruct((256, 2048), BF16),
+            jax.ShapeDtypeStruct((TB, 2048), F32),
+        ),
+        in_specs=[ANY, VMEM],
+        out_specs=(ANY, VMEM),
+        scratch_shapes=[pltpu.VMEM((256, 2048), BF16), pltpu.SemaphoreType.DMA((2, 4))],
+        name="finish",
+    )(signal, pieces)
+
+
+def fused(raw, mask, taps, blocks, owners, geo):
     dma = pltpu.SemaphoreType.DMA
     return pl.pallas_call(
         kernel,
         out_shape=(
             jax.ShapeDtypeStruct((256, 2048), BF16),
-            jax.ShapeDtypeStruct((N, TB, TB), BF16),
+            jax.ShapeDtypeStruct((24, TB, TB), BF16),
         ),
-        in_specs=[VMEM, VMEM, VMEM, VMEM, ANY],
+        in_specs=[ANY, VMEM, VMEM, VMEM, VMEM, ANY],
         out_specs=(ANY, VMEM),
         scratch_shapes=[
+            pltpu.VMEM((256, 2048), BF16),
+            pltpu.VMEM((24, 2 * TB), F32),
+            pltpu.VMEM((8, TB), jnp.int32),
             pltpu.VMEM((2, 256, TB), BF16),
             pltpu.VMEM((2, 16, 2048), BF16),
             pltpu.VMEM((2, 256, TB), BF16),
@@ -405,39 +557,42 @@
             pltpu.VMEM((33 * TB, 2 * TB), BF16),
             pltpu.VMEM((ROWS, TB), F32),
             pltpu.VMEM((N, 256, TB), BF16),
-            pltpu.VMEM((N, 256, TB), BF16),
+            pltpu.VMEM((2, 8, 256, TB), BF16),
             pltpu.VMEM((N, 8, TB), F32),
-            pltpu.VMEM((N, 8, TB), F32),
+            pltpu.VMEM((2, 8, 8, TB), F32),
             pltpu.VMEM((4096, TB), BF16),
             pltpu.VMEM((N, TB, 256), BF16),
-            pltpu.VMEM((4, N, TB, 1024), BF16),
+            pltpu.VMEM((2, N, TB, 2048), BF16),
             pltpu.VMEM((N, TB, TB), F32),
-            pltpu.VMEM((N, TB, TB), BF16),
-            pltpu.VMEM((N, TB, TB), BF16),
+            pltpu.VMEM((2, N, TB, TB), BF16),
+            pltpu.VMEM((24, TB, TB), BF16),
             dma((8,)),
             dma((8,)),
             dma((N,)),
+            dma((2, 8)),
             dma((N,)),
-            dma((N,)),
-            dma((N,)),
-            dma((N,)),
-            dma((N,)),
-            dma((3,)),
+            dma((2, 8)),
+            dma((2, N)),
+            dma((24,)),
+            dma((4,)),
         ],
         compiler_params=pltpu.CompilerParams(
             vmem_limit_bytes=56 << 20, collective_id=0, has_side_effects=True
         ),
         name="fused",
-    )(raw, mask, taps, roi, geo)
+    )(raw, mask, taps, blocks, owners, geo)
 
 
 def shards(raw, chan_mask, kernel_rows, geometry, roi_block, roi_owner):
-    taps = jnp.zeros((24, 2 * TB), F32).at[:21].set(kernel_rows[0].astype(F32))
-    slots = roi_block.shape[0]
-    roi = jnp.full((2, TB), -1, jnp.int32).at[:, :slots].set(jnp.stack([roi_block, roi_owner]))
-    signal, pieces = fused(raw, chan_mask.reshape(1, 256), taps, roi, geometry.reshape(4096, TB))
-    image = pieces.transpose(1, 0, 2).reshape(TB, 2048).astype(F32)
-    return (signal, image)
+    signal, pieces = fused(
+        raw,
+        chan_mask.reshape(1, 256),
+        kernel_rows[0],
+        roi_block.reshape(1, -1),
+        roi_owner.reshape(1, -1),
+        geometry.reshape(4096, TB),
+    )
+    return finish(signal, pieces)
 
 
 def solution(mesh):

time: 62.3 us -> 58.2 us (0.934)
  the two profiles are of different devices: /device:TPU:64 before, /device:TPU:25 now
where the time goes in v3:
time: 58.2 us; the launch traced here: 58 us
  Pallas kernels  57.4 us (99%)
  between operations  0.64 us (1%)
    pallas_call x1, Pallas kernels, fused(): pl.pallas_call(kernel, out_shape=(jax.ShapeDtypeStruct((256, 2048), BF16)...  53.3 us
    pallas_call x1, Pallas kernels, finish(): pl.pallas_call(finish_kernel, out_shape=(jax.ShapeDtypeStruct((256, 2048)...  4.08 us

profile of v3, /device:TPU:25, one launch (start us, length us, event | category | flops | bytes accessed | tf_op | source)
XLA Modules:
  0.0 58.0 jit_solution(17402813651084958066)
XLA Ops:
  0.6 53.3 %fused.1 = (bf16[256,2048]{1,0:T(8,128)(2,1)}, bf16[24,128,128]{2,1,0:T(8,128)(2,1)}) custom-call(bf16[256,2048]{1,0:T(8,128)(2,1)} %raw_hbm.1, s32[1,256]{1,0:T(1,128)} %bitcast.7, bf16[21,256]{1,0:T(8,128)(2,1)} %bitcast.6, s32[1,102]{1,0:T(1,128)} %bitcast.8, s32[1,102]{1,0:T(1,128)} %bitcast.9, bf16[4096,128]{1,0:T(8,128)(2,1)} %bitcast.5), custom_call_target="tpu_custom_call" | custom-call | tf_op jit(solution)/shard_map/fused/pallas_call | solution.py:537
  53.9 4.1 %finish.1 = (bf16[256,2048]{1,0:T(8,128)(2,1)}, f32[128,2048]{1,0:T(8,128)}) custom-call(bf16[256,2048]{1,0:T(8,128)(2,1)} %get-tuple-element.4.signal_ref, bf16[24,128,128]{2,1,0:T(8,128)(2,1)} %get-tuple-element.5.piece_ref), custom_call_target="tpu_custom_call" | custom-call | tf_op jit(solution)/shard_map/finish/pallas_call | solution.py:522

commit v4 on v3

v4 whole, which is shorter than its diff:
```python
import jax
import jax.numpy as jnp
from jax import lax
from jax.experimental import pallas as pl
from jax.experimental.pallas import tpu as pltpu
from jax.sharding import PartitionSpec as P

TB = 128
N = 16
CHUNK = 64
ROWS = CHUNK * 16
BLOCKS = 22
UNROLL = BLOCKS
LIMIT = 56 << 20
MESH = pl.DeviceIdType.MESH
VMEM = pl.BlockSpec(memory_space=pltpu.VMEM)
ANY = pl.BlockSpec(memory_space=pl.ANY)
HBM = pl.BlockSpec(memory_space=pltpu.HBM)
BF16 = jnp.bfloat16
F32 = jnp.float32


def row_of(ref, index, size):
    return ref.at[pl.ds(pl.multiple_of(index, size), size)]


def build_bands(taps_ref, band_ref):
    row = lax.broadcasted_iota(jnp.int32, (TB, TB), 0)
    col = lax.broadcasted_iota(jnp.int32, (TB, TB), 1)
    upper = col >= row
    zero = jnp.zeros((TB, TB), F32)

    def pair(m, carry):
        for p in range(2):
            taps = taps_ref[pl.ds(2 * m + p, 1), :]
            low, high = [
                pltpu.roll(
                    jnp.broadcast_to(taps[:, half * TB : (half + 1) * TB], (TB, TB)),
                    0,
                    1,
                    stride=1,
                    stride_axis=0,
                )
                for half in range(2)
            ]
            pieces = (
                jnp.where(upper, zero, high),
                jnp.where(upper, high, low),
                jnp.where(upper, low, zero),
            )
            for piece in range(3):
                start = pl.multiple_of((m * 3 + piece) * TB, TB)
                band_ref[pl.ds(start, TB), p * TB : (p + 1) * TB] = pieces[piece].astype(BF16)
        return carry

    lax.fori_loop(0, 11, pair, 0)


def kernel(
    raw_hbm,
    mask_ref,
    taps_ref,
    block_ref,
    owner_ref,
    geo_ref,
    signal_ref,
    image_ref,
    raw_ref,
    taps,
    roi_ref,
    edge_t,
    edge_w,
    halo_t,
    halo_w,
    halo_c,
    mask_col,
    tall,
    shifted,
    band,
    sums,
    sig,
    recv_0,
    recv_1,
    own_out,
    own_in,
    geo,
    plan_v,
    plan,
    runs,
    piece_out,
    piece_in,
    halo_send,
    halo_recv,
    own_send,
    own_recv,
    tile_send,
    tile_recv,
    image_send,
    image_recv,
    local,
):
    plane, wire, tick = lax.axis_index("plane"), lax.axis_index("wire"), lax.axis_index("tick")
    me = plane * 4 + wire
    recv = (recv_0, recv_1)
    half, inner = wire // 2, lax.rem(wire, 2)
    spot = plane * 2 + inner
    whole = jnp.logical_or(wire == 1, wire == 2)
    split = jnp.logical_not(whole)
    mine = plane * 2 + half
    up_t, down_t = lax.rem(tick + 1, 16), lax.rem(tick + 15, 16)
    up_w, down_w = lax.rem(wire + 1, 4), lax.rem(wire + 3, 4)

    def member(m):
        return (m // 4, lax.rem(m, 4), tick)

    barrier = pltpu.get_barrier_semaphore()

    def greet(r, carry):
        pl.semaphore_signal(barrier, inc=1, device_id=member(lax.rem(me + r, N)), device_id_type=MESH)
        return carry

    has = {"t+": tick < 15, "t-": tick > 0, "w+": wire < 3, "w-": wire > 0}

    def when_all(keys, action):
        test = has[keys[0]]
        for key in keys[1:]:
            test = jnp.logical_and(test, has[key])
        pl.when(test)(action)
        return test

    for t_key, t in (("t+", up_t), ("t-", down_t)):
        for w_keys, w in (((), wire), (("w+",), up_w), (("w-",), down_w)):

            def greet_side():
                pl.semaphore_signal(barrier, inc=1, device_id=(plane, w, t), device_id_type=MESH)

            when_all((t_key, *w_keys), greet_side)
    lax.fori_loop(1, N, greet, 0)

    raw_copy = pltpu.make_async_copy(raw_hbm, raw_ref, local.at[3])
    raw_copy.start()
    geo_copy = pltpu.make_async_copy(geo_ref, geo, local.at[0])
    geo_copy.start()
    taps[...] = jnp.zeros((24, 2 * TB), F32)
    taps[0:21, :] = taps_ref[...].astype(F32)
    roi_ref[...] = jnp.full((8, TB), -1, jnp.int32)
    roi_ref[0:1, 0:102] = block_ref[...]
    roi_ref[1:2, 0:102] = owner_ref[...]

    row = lax.broadcasted_iota(jnp.int32, (256, 256), 0)
    col = lax.broadcasted_iota(jnp.int32, (256, 256), 1)
    diag = jnp.where(row == col, mask_ref[...].astype(F32), 0.0).astype(BF16)
    mask_col[...] = jnp.dot(diag, jnp.ones((256, TB), BF16), preferred_element_type=F32)

    r = lax.broadcasted_iota(jnp.int32, (TB, TB), 0)
    hit = jnp.where(roi_ref[0:1, :] == lax.rem(r, 8) * 16 + r // 8, roi_ref[1:2, :] + 1, 0)
    table = jnp.dot(hit.astype(F32).astype(BF16), jnp.ones((TB, TB), BF16), preferred_element_type=F32)
    own_out[...] = table.reshape(N, 8, TB)

    raw_copy.wait()
    for side, start in ((0, 0), (1, 15 * TB)):
        edge_t[side] = (raw_ref[:, start : start + TB].astype(F32) * mask_col[...]).astype(BF16)
    for side, start in ((0, 0), (1, 240)):
        for j in range(N):
            cols = slice(j * TB, (j + 1) * TB)
            edge_w[side, :, cols] = (
                raw_ref[start : start + 16, cols].astype(F32) * mask_col[start : start + 16, :]
            ).astype(BF16)

    ticks_near = (tick < 15).astype(jnp.int32) + (tick > 0).astype(jnp.int32)
    wires_near = 1 + (wire < 3).astype(jnp.int32) + (wire > 0).astype(jnp.int32)
    pl.semaphore_wait(barrier, 15 + ticks_near * wires_near)

    first, last = slice(0, TB), slice(15 * TB, 16 * TB)
    halo_copies = [
        pltpu.make_async_remote_copy(
            src_ref=src,
            dst_ref=dst,
            send_sem=halo_send.at[i],
            recv_sem=halo_recv.at[i],
            device_id=(plane, w, t),
            device_id_type=MESH,
        )
        for i, (src, dst, w, t) in enumerate(
            (
                (edge_t.at[1], halo_t.at[0], wire, up_t),
                (edge_t.at[0], halo_t.at[1], wire, down_t),
                (edge_w.at[1], halo_w.at[0], up_w, tick),
                (edge_w.at[0], halo_w.at[1], down_w, tick),
                (edge_w.at[1, :, last], halo_c.at[0], up_w, up_t),
                (edge_w.at[1, :, first], halo_c.at[1], up_w, down_t),
                (edge_w.at[0, :, last], halo_c.at[2], down_w, up_t),
                (edge_w.at[0, :, first], halo_c.at[3], down_w, down_t),
            )
        )
    ]
    outward = (("t+",), ("t-",), ("w+",), ("w-",), ("w+", "t+"), ("w+", "t-"), ("w-", "t+"), ("w-", "t-"))
    inward = (("t-",), ("t+",), ("w-",), ("w+",), ("w-", "t-"), ("w-", "t+"), ("w+", "t-"), ("w+", "t+"))
    landing = [halo_t.at[0], halo_t.at[1], halo_w.at[0], halo_w.at[1]] + [halo_c.at[i] for i in range(4)]
    for keys, copy in zip(outward, halo_copies):
        when_all(keys, copy.start)

    def take_halo(i):
        test = when_all(inward[i], halo_copies[i].wait_recv)

        @pl.when(jnp.logical_not(test))
        def _():
            landing[i][...] = jnp.zeros(landing[i].shape, BF16)

    def to_whole(r, turn, src, dst, send, receive):
        a = lax.rem(mine + r, 8)
        return pltpu.make_async_remote_copy(
            src_ref=src(a),
            dst_ref=dst(turn, spot),
            send_sem=send.at[a],
            recv_sem=receive.at[turn, spot],
            device_id=(a // 2, 1 + lax.rem(a, 2), tick),
            device_id_type=MESH,
        )

    def to_split(p, h, src, dst, send, receive):
        return pltpu.make_async_remote_copy(
            src_ref=src(8 + 2 * p + h),
            dst_ref=dst(h, spot),
            send_sem=send.at[8 + 2 * p + h],
            recv_sem=receive.at[h, spot],
            device_id=(p, 3 * half, tick),
            device_id_type=MESH,
        )

    def exchange(act, *refs):
        def across(i, carry):
            act(to_whole(2 * i + 1, 1, *refs))
            return carry

        def within(i, carry):
            act(to_whole(2 * i, 0, *refs))
            return carry

        def splits(r, carry):
            for h in range(2):
                act(to_split(lax.rem(plane + r, 4), h, *refs))
            return carry

        lax.fori_loop(0, 4, across, 0)
        lax.fori_loop(1, 4, within, 0)
        lax.fori_loop(1, 4, splits, 0)

        @pl.when(split)
        def _():
            act(to_whole(0, 0, *refs))

        @pl.when(whole)
        def _():
            for h in range(2):
                act(to_split(plane, h, *refs))

    def begin(copy):
        copy.start()

    def wait_send(copy):
        copy.wait_send()

    def side_of(turn):
        return jnp.where(whole, 1 - half, half) if turn else half

    def arrival(h, other, dst, receive):
        return pltpu.make_async_remote_copy(
            src_ref=dst(h, other),
            dst_ref=dst(h, other),
            send_sem=receive.at[h, other],
            recv_sem=receive.at[h, other],
            device_id=(other // 2, 2 * side_of(h) + lax.rem(other, 2), tick),
            device_id_type=MESH,
        )

    def wait_half(h, second, dst, receive):
        def one(r, carry):
            arrival(h, lax.rem(spot + r, 8), dst, receive).wait_recv()
            return carry

        lax.fori_loop(1, 8, one, 0)
        if second:

            @pl.when(whole)
            def _():
                arrival(h, spot, dst, receive).wait_recv()

    own_refs = (lambda j: own_out.at[j], lambda h, i: own_in.at[h, i], own_send, own_recv)
    exchange(begin, *own_refs)

    @pl.when(whole)
    def _():
        own_in[0, spot] = own_out[mine]

    @pl.when(split)
    def _():
        for h in range(2):
            own_in[h, spot] = own_out[8 + 2 * plane + h]

    build_bands(taps, band)

    def spread(i, carry):
        wires = pl.ds(pl.multiple_of(i * 16, 16), 16)
        keep = mask_col[wires, :]
        for j in range(N):
            piece = raw_ref[wires, j * TB : (j + 1) * TB].astype(F32) * keep
            tall[pl.ds((i + 1) * 288 + j + 1, 16, stride=18), :] = piece
        return carry

    lax.fori_loop(0, 16, spread, 0)

    def window(i, carry):
        for u in range(8):
            slot = i * 8 + u
            for piece in range(3):
                shifted[piece, slot] = tall[pl.ds(slot * 18 + piece, 16), :].astype(BF16)
        return carry

    for i in (0, 1):
        take_halo(i)

    def spread_ticks(i, carry):
        wires = pl.ds(pl.multiple_of(i * 16, 16), 16)
        for side, j in ((0, 0), (1, 17)):
            tall[pl.ds((i + 1) * 288 + j, 16, stride=18), :] = halo_t[side, wires, :].astype(F32)
        return carry

    lax.fori_loop(0, 16, spread_ticks, 0)
    lax.fori_loop(2, 34, window, 0)

    def run_chunk(c):
        base = c * CHUNK
        lhs = jnp.concatenate(
            [
                shifted[piece, pl.ds(base + 6 + 2 * m, CHUNK + 1)].reshape((CHUNK + 1) * 16, TB)
                for m in range(11)
                for piece in range(3)
            ],
            axis=1,
        )
        both = jnp.dot(lhs, band[...], preferred_element_type=F32)
        sums[...] = both[:ROWS, :TB] + both[16:, TB:]
        for j in range(N):
            for b in range(CHUNK // 16):
                sig[j, c * 2 + b // 2, (b % 2) * 16 : (b % 2) * 16 + 16, :] = sums[pl.ds(b * 256 + j, 16, stride=16), :].astype(BF16)

        exchange(
            begin,
            lambda j: sig.at[j, pl.ds(c * 2, 2)],
            lambda h, i: recv[h].at[pl.ds(i * 8 + c * 2, 2)],
            tile_send,
            tile_recv,
        )

    def middle(i, carry):
        run_chunk(i + 1)
        return carry

    lax.fori_loop(0, 2, middle, 0)

    for i in range(2, 8):
        take_halo(i)
    for side, base in ((0, 0), (1, 272 * 18)):
        for j in range(N):
            tall[pl.ds(base + j + 1, 16, stride=18), :] = halo_w[side, :, j * TB : (j + 1) * TB].astype(F32)
        for t, j in ((0, 0), (1, 17)):
            tall[pl.ds(base + j, 16, stride=18), :] = halo_c[side * 2 + t].astype(F32)
    lax.fori_loop(0, 2, window, 0)
    lax.fori_loop(34, 36, window, 0)

    def outer(i, carry):
        run_chunk(i * 3)
        return carry

    lax.fori_loop(0, 2, outer, 0)

    def store_signal(j, carry):
        pltpu.make_async_copy(
            sig.at[j], signal_ref.at[:, :, pl.ds(pl.multiple_of(j * TB, TB), TB)], local.at[1]
        ).start()
        return carry

    lax.fori_loop(0, N, store_signal, 0)

    @pl.when(whole)
    def _():
        recv[0][pl.ds(spot * 8, 8)] = sig[mine]

    @pl.when(split)
    def _():
        for h in range(2):
            recv[h][pl.ds(spot * 8, 8)] = sig[8 + 2 * plane + h]

    own_dst, tile_dst = own_refs[1], lambda h, i: recv[h].at[pl.ds(i * 8, 8)]
    wait_half(0, False, own_dst, own_recv)
    wait_half(1, True, own_dst, own_recv)

    tile = lax.broadcasted_iota(jnp.int32, (64, TB), 0)
    lane = lax.broadcasted_iota(jnp.int32, (64, TB), 1)
    place = lax.broadcasted_iota(jnp.int32, (64, 2 * TB), 1).astype(F32)
    before = (lax.broadcasted_iota(jnp.int32, (64, 64), 1) < lax.broadcasted_iota(jnp.int32, (64, 64), 0)).astype(
        F32
    )
    lower = (lax.broadcasted_iota(jnp.int32, (TB, TB), 0) < lax.broadcasted_iota(jnp.int32, (TB, TB), 1)).astype(
        F32
    )
    for h in range(2):
        side = side_of(h)
        georow = ((tile // 16) * 4 + 2 * side + lax.rem(tile // 8, 2)) * 8 + lax.rem(tile, 8)
        wanted = own_in[h].reshape(64, TB)
        member_of = jnp.where(wanted == (lane + 1).astype(F32), 1.0, 0.0)
        rank = jnp.dot(before.astype(BF16), member_of.astype(BF16), preferred_element_type=F32)
        count = jnp.sum(member_of, axis=0, keepdims=True)
        blocks = jnp.floor((count + 7.0) * 0.125)
        opening = jnp.dot(
            jnp.broadcast_to(blocks, (8, TB)).astype(BF16), lower.astype(BF16), preferred_element_type=F32
        )[0:1, :]
        found = jnp.sum(member_of, axis=1, keepdims=True)
        spot_of = jnp.sum(member_of * (opening * 8.0 + rank), axis=1, keepdims=True) - (1.0 - found)
        rank_of = jnp.sum(member_of * rank, axis=1, keepdims=True)
        here = jnp.where(spot_of == place, 1.0, 0.0)
        tile_f, geo_f = tile[:, 0:1].astype(F32), georow[:, 0:1].astype(F32)
        plan_v[h, 0:1, :] = (64.0 + jnp.sum(here * (tile_f - 64.0), axis=0, keepdims=True)).astype(jnp.int32)
        plan_v[h, 1:2, :] = jnp.sum(here * geo_f, axis=0, keepdims=True).astype(jnp.int32)
        again = jnp.where(spot_of == place * 8.0, 1.0, 0.0) * jnp.where(rank_of > 0.0, 1.0, 0.0)
        plan_v[h, 2:3, :] = jnp.sum(again, axis=0, keepdims=True).astype(jnp.int32)
        closing = jnp.where(count > 0.0, opening + blocks - 1.0, float(BLOCKS))
        plan_v[h, 3:4, 0:TB] = closing.astype(jnp.int32)
        plan_v[h, 3:4, TB : 2 * TB] = closing.astype(jnp.int32)
        plan_v[h, 4:8, :] = jnp.zeros((4, 2 * TB), jnp.int32)
        recv[h][64] = jnp.zeros((32, TB), BF16)
        runs[h, BLOCKS] = jnp.zeros((TB, TB), F32)
    plan_copy = pltpu.make_async_copy(plan_v, plan, local.at[2])
    plan_copy.start()
    geo_copy.wait()
    plan_copy.wait()

    def image_slot(p, w, h, k):
        outer = jnp.logical_or(w == 0, w == 3)
        return jnp.where(outer, 8 + (2 * p + k) * 2 + h, 2 * p + h)

    def image_copy(k, o):
        slot = image_slot(plane, wire, half, k)
        return pltpu.make_async_remote_copy(
            src_ref=piece_out.at[k, o],
            dst_ref=piece_in.at[slot],
            send_sem=image_send.at[k, o],
            recv_sem=image_recv.at[slot],
            device_id=member(o),
            device_id_type=MESH,
        )

    both_halves = jnp.where(whole, 1.0, 0.0)
    for h in range(2):
        k = 0 if h == 0 else jnp.where(whole, 0, 1)
        wait_half(h, h == 1, tile_dst, tile_recv)

        def block(b, run):
            lhs = jnp.concatenate([geo[jnp.clip(plan[h, 1, b * 8 + i], 0, TB - 1)] for i in range(8)], axis=0)
            rhs = jnp.concatenate([recv[h][jnp.clip(plan[h, 0, b * 8 + i], 0, 64)] for i in range(8)], axis=0)
            part = lax.dot_general(lhs, rhs, (((0,), (0,)), ((), ())), preferred_element_type=F32)
            run = run * plan[h, 2, b].astype(F32) + part
            runs[h, b] = run
            return run

        lax.fori_loop(0, BLOCKS, block, jnp.zeros((TB, TB), F32), unroll=UNROLL)

        for i in range(N):
            o = lax.rem(me + 1 + i, N)

            def send_piece():
                now = runs[h, jnp.clip(plan[h, 3, o], 0, BLOCKS)]
                if h == 1:
                    now = now + runs[0, jnp.clip(plan[0, 3, o], 0, BLOCKS)] * both_halves
                piece_out[k, o] = now.astype(BF16)
                if i < N - 1:
                    image_copy(k, o).start()
                else:
                    piece_in[image_slot(plane, wire, half, k)] = piece_out[k, o]

            if h == 0:
                pl.when(split)(send_piece)
            else:
                send_piece()

    for keys, copy in zip(outward, halo_copies):
        when_all(keys, copy.wait_send)
    exchange(wait_send, *own_refs)
    exchange(wait_send, lambda j: sig.at[j], tile_dst, tile_send, tile_recv)
    pltpu.make_async_copy(signal_ref, signal_ref, local.at[1]).wait()

    def wait_image_send(k):
        def one(r, carry):
            image_copy(k, lax.rem(me + r, N)).wait_send()
            return carry

        lax.fori_loop(1, N, one, 0)

    wait_image_send(0)

    @pl.when(split)
    def _():
        wait_image_send(1)

    def image_arrival(slot):
        return pltpu.make_async_remote_copy(
            src_ref=piece_in.at[slot],
            dst_ref=piece_in.at[slot],
            send_sem=image_recv.at[slot],
            recv_sem=image_recv.at[slot],
            device_id=(plane, up_w, tick),
            device_id_type=MESH,
        )

    def hand_out(slot):
        pltpu.make_async_copy(piece_in.at[slot], image_ref.at[slot], local.at[4]).start()

    def landed(slot):
        image_arrival(slot).wait_recv()
        hand_out(slot)

    def whole_images(r, carry):
        landed(lax.rem(mine + r, 8))
        return carry

    def split_images(r, carry):
        for k in range(2):
            for h in range(2):
                landed(8 + (2 * lax.rem(plane + r, 4) + k) * 2 + h)
        return carry

    lax.fori_loop(1, 8, whole_images, 0)
    lax.fori_loop(1, 4, split_images, 0)
    for k in range(2):
        landed(8 + (2 * plane + k) * 2 + 1 - half)

    @pl.when(split)
    def _():
        landed(mine)
        for k in range(2):
            hand_out(8 + (2 * plane + k) * 2 + half)

    @pl.when(whole)
    def _():
        hand_out(mine)
        for k in range(2):
            landed(8 + (2 * plane + k) * 2 + half)

    pltpu.make_async_copy(piece_in, image_ref, local.at[4]).wait()


def finish_kernel(signal_ref, piece_ref, signal_out, image_ref, held, pieces, image, sem):
    loads, stores = [], []
    for g in range(4):
        span = pl.ds(2 * g, 2)
        loads.append(
            (
                pltpu.make_async_copy(piece_ref.at[span], pieces.at[span], sem.at[0, g]),
                pltpu.make_async_copy(
                    piece_ref.at[pl.ds(8 + 4 * g, 4)], pieces.at[pl.ds(8 + 4 * g, 4)], sem.at[1, g]
                ),
                pltpu.make_async_copy(signal_ref.at[span], held.at[span], sem.at[2, g]),
            )
        )
        low, high = pl.ds(2 * g * TB, 2 * TB), pl.ds((8 + 2 * g) * TB, 2 * TB)
        stores.append(
            (
                pltpu.make_async_copy(image.at[:, low], image_ref.at[:, low], sem.at[3, g]),
                pltpu.make_async_copy(image.at[:, high], image_ref.at[:, high], sem.at[4, g]),
                pltpu.make_async_copy(held.at[span], signal_out.at[span], sem.at[5, g]),
            )
        )
    for load in loads:
        for copy in load:
            copy.start()
    for g in range(4):
        loads[g][0].wait()
        loads[g][1].wait()
        for j in (2 * g, 2 * g + 1):
            image[:, j * TB : (j + 1) * TB] = pieces[j].astype(F32)
            image[:, (8 + j) * TB : (9 + j) * TB] = pieces[8 + 2 * j].astype(F32) + pieces[
                9 + 2 * j
            ].astype(F32)
        stores[g][0].start()
        stores[g][1].start()
        loads[g][2].wait()
        stores[g][2].start()
    for store in stores:
        for copy in store:
            copy.wait()


def finish(signal, pieces):
    return pl.pallas_call(
        finish_kernel,
        out_shape=(
            jax.ShapeDtypeStruct((8, 32, 2048), BF16),
            jax.ShapeDtypeStruct((TB, 2048), F32),
        ),
        in_specs=[ANY, ANY],
        out_specs=(ANY, ANY),
        scratch_shapes=[
            pltpu.VMEM((8, 32, 2048), BF16),
            pltpu.VMEM((24, TB, TB), BF16),
            pltpu.VMEM((TB, 2048), F32),
            pltpu.SemaphoreType.DMA((6, 4)),
        ],
        compiler_params=pltpu.CompilerParams(vmem_limit_bytes=8 << 20),
        name="finish",
    )(signal, pieces)


def fused(raw, mask, taps, blocks, owners, geo):
    dma = pltpu.SemaphoreType.DMA
    return pl.pallas_call(
        kernel,
        out_shape=(
            jax.ShapeDtypeStruct((8, 32, 2048), BF16),
            jax.ShapeDtypeStruct((24, TB, TB), BF16),
        ),
        in_specs=[HBM, VMEM, VMEM, VMEM, VMEM, HBM],
        out_specs=(ANY, ANY),
        scratch_shapes=[
            pltpu.VMEM((256, 2048), BF16),
            pltpu.VMEM((24, 2 * TB), F32),
            pltpu.VMEM((8, TB), jnp.int32),
            pltpu.VMEM((2, 256, TB), BF16),
            pltpu.VMEM((2, 16, 2048), BF16),
            pltpu.VMEM((2, 256, TB), BF16),
            pltpu.VMEM((2, 16, 2048), BF16),
            pltpu.VMEM((4, 16, TB), BF16),
            pltpu.VMEM((256, TB), F32),
            pltpu.VMEM((288 * 18, TB), F32),
            pltpu.VMEM((3, 288, 16, TB), BF16),
            pltpu.VMEM((33 * TB, 2 * TB), BF16),
            pltpu.VMEM((ROWS, TB), F32),
            pltpu.VMEM((N, 8, 32, TB), BF16),
            pltpu.VMEM((65, 32, TB), BF16),
            pltpu.VMEM((65, 32, TB), BF16),
            pltpu.VMEM((N, 8, TB), F32),
            pltpu.VMEM((2, 8, 8, TB), F32),
            pltpu.VMEM((TB, 32, TB), BF16),
            pltpu.VMEM((2, 8, 2 * TB), jnp.int32),
            pltpu.SMEM((2, 8, 2 * TB), jnp.int32),
            pltpu.VMEM((2, BLOCKS + 1, TB, TB), F32),
            pltpu.VMEM((2, N, TB, TB), BF16),
            pltpu.VMEM((24, TB, TB), BF16),
            dma((8,)),
            dma((8,)),
            dma((N,)),
            dma((2, 8)),
            dma((N,)),
            dma((2, 8)),
            dma((2, N)),
            dma((24,)),
            dma((5,)),
        ],
        compiler_params=pltpu.CompilerParams(
            vmem_limit_bytes=LIMIT, collective_id=0, has_side_effects=True
        ),
        name="fused",
    )(raw, mask, taps, blocks, owners, geo)


def shards(raw, chan_mask, kernel_rows, geometry, roi_block, roi_owner):
    signal, pieces = fused(
        raw,
        chan_mask.reshape(1, 256),
        kernel_rows[0],
        roi_block.reshape(1, -1),
        roi_owner.reshape(1, -1),
        geometry,
    )
    signal, image = finish(signal, pieces)
    return (signal.reshape(256, 2048), image)


def solution(mesh):
    in_specs = (
        P(("plane", "wire"), "tick"),
        P(("plane", "wire")),
        P("plane", None, None),
        P(),
        P(("plane", "wire", "tick")),
        P(("plane", "wire", "tick")),
    )
    out_specs = (P(("plane", "wire"), "tick"), P(("plane", "wire"), "tick"))
    return jax.shard_map(shards, mesh=mesh, in_specs=in_specs, out_specs=out_specs, check_vma=False)
```

time: 58.2 us -> 55.4 us (0.952)
  Pallas kernels: 57.4 us -> 52.2 us
  local copies, waits for them, and re-layouts: 0 us -> 2.35 us
    pallas_call x2, Pallas kernels: 57.4 us -> 52.2 us  [the longest x1 49.6 us: fused(): pl.pallas_call(kernel, out_shape=(jax.ShapeDtypeStruct((8, 32, 2048), BF1...]
    unnamed x0 -> x4, local copies, waits for them, and re-layouts: none -> 2.35 us
where the time goes in v4:
time: 55.4 us; the launch traced here: 55.2 us
  Pallas kernels  52.2 us (94%)
  local copies, waits for them, and re-layouts  2.35 us (4%)
  between operations  0.65 us (1%)
    pallas_call x1, Pallas kernels, fused(): pl.pallas_call(kernel, out_shape=(jax.ShapeDtypeStruct((8, 32, 2048), BF1...  49.6 us
    pallas_call x1, Pallas kernels, finish(): pl.pallas_call(finish_kernel, out_shape=(jax.ShapeDtypeStruct((8, 32, 204...  2.6 us
    unnamed x4, local copies, waits for them, and re-layouts  2.35 us

profile of v4, /device:TPU:25, one launch (start us, length us, event | category | flops | bytes accessed | tf_op | source)
XLA Modules:
  0.0 55.2 jit_solution(10980373333815995578)
XLA Ops:
  0.6 49.6 %fused.1 = (bf16[8,32,2048]{2,1,0:T(8,128)(2,1)}, bf16[24,128,128]{2,1,0:T(8,128)(2,1)}) custom-call(bf16[256,2048]{1,0:T(8,128)(2,1)} %raw_hbm.1, s32[1,256]{1,0:T(1,128)} %bitcast.6, bf16[21,256]{1,0:T(8,128)(2,1)} %bitcast.5, s32[1,102]{1,0:T(1,128)} %bitcast.7, s32[1,102]{1,0:T(1,128)} %bitcast.8, bf16[128,32,128]{2,1,0:T(8,128)(2,1)} %geo_ref.1), custom_call_target="tpu_custom_call" | custom-call | tf_op jit(solution)/shard_map/fused/pallas_call | solution.py:616
  50.2 0.0 copy-start
  50.3 1.2 %copy-done = bf16[8,32,2048]{2,1,0:T(8,128)(2,1)S(1)} copy-done((bf16[8,32,2048]{2,1,0:T(8,128)(2,1)S(1)}, bf16[8,32,2048]{2,1,0:T(8,128)(2,1)}, u32[]{:S(2)}) %copy-start) | copy-done | bytes 1048600
  51.5 0.0 copy-start.1
  51.5 1.1 %copy-done.1 = bf16[24,128,128]{2,1,0:T(8,128)(2,1)S(1)} copy-done((bf16[24,128,128]{2,1,0:T(8,128)(2,1)S(1)}, bf16[24,128,128]{2,1,0:T(8,128)(2,1)}, u32[]{:S(2)}) %copy-start.1) | copy-done | bytes 786456
  52.6 2.6 %finish.1 = (bf16[8,32,2048]{2,1,0:T(8,128)(2,1)}, f32[128,2048]{1,0:T(8,128)}) custom-call(bf16[8,32,2048]{2,1,0:T(8,128)(2,1)S(1)} %copy-done, bf16[24,128,128]{2,1,0:T(8,128)(2,1)S(1)} %copy-done.1), custom_call_target="tpu_custom_call" | custom-call | tf_op jit(solution)/shard_map/finish/pallas_call | solution.py:595
Async XLA Ops:
  50.2 1.2 %copy-start = (bf16[8,32,2048]{2,1,0:T(8,128)(2,1)S(1)}, bf16[8,32,2048]{2,1,0:T(8,128)(2,1)}, u32[]{:S(2)}) copy-start(bf16[8,32,2048]{2,1,0:T(8,128)(2,1)} %get-tuple-element.6.signal_ref) | copy-start | bytes 3145732
  51.5 1.1 %copy-start.1 = (bf16[24,128,128]{2,1,0:T(8,128)(2,1)S(1)}, bf16[24,128,128]{2,1,0:T(8,128)(2,1)}, u32[]{:S(2)}) copy-start(bf16[24,128,128]{2,1,0:T(8,128)(2,1)} %get-tuple-element.7.piece_ref) | copy-start | bytes 2359300

commit v5 on v4

--- a/solution.py
+++ b/solution.py
@@ -140,7 +140,6 @@
     raw_copy = pltpu.make_async_copy(raw_hbm, raw_ref, local.at[3])
     raw_copy.start()
     geo_copy = pltpu.make_async_copy(geo_ref, geo, local.at[0])
-    geo_copy.start()
     taps[...] = jnp.zeros((24, 2 * TB), F32)
     taps[0:21, :] = taps_ref[...].astype(F32)
     roi_ref[...] = jnp.full((8, TB), -1, jnp.int32)
@@ -152,12 +151,8 @@
     diag = jnp.where(row == col, mask_ref[...].astype(F32), 0.0).astype(BF16)
     mask_col[...] = jnp.dot(diag, jnp.ones((256, TB), BF16), preferred_element_type=F32)
 
-    r = lax.broadcasted_iota(jnp.int32, (TB, TB), 0)
-    hit = jnp.where(roi_ref[0:1, :] == lax.rem(r, 8) * 16 + r // 8, roi_ref[1:2, :] + 1, 0)
-    table = jnp.dot(hit.astype(F32).astype(BF16), jnp.ones((TB, TB), BF16), preferred_element_type=F32)
-    own_out[...] = table.reshape(N, 8, TB)
-
     raw_copy.wait()
+    geo_copy.start()
     for side, start in ((0, 0), (1, 15 * TB)):
         edge_t[side] = (raw_ref[:, start : start + TB].astype(F32) * mask_col[...]).astype(BF16)
     for side, start in ((0, 0), (1, 240)):
@@ -286,18 +281,6 @@
             def _():
                 arrival(h, spot, dst, receive).wait_recv()
 
-    own_refs = (lambda j: own_out.at[j], lambda h, i: own_in.at[h, i], own_send, own_recv)
-    exchange(begin, *own_refs)
-
-    @pl.when(whole)
-    def _():
-        own_in[0, spot] = own_out[mine]
-
-    @pl.when(split)
-    def _():
-        for h in range(2):
-            own_in[h, spot] = own_out[8 + 2 * plane + h]
-
     build_bands(taps, band)
 
     def spread(i, carry):
@@ -327,53 +310,73 @@
         return carry
 
     lax.fori_loop(0, 16, spread_ticks, 0)
-    lax.fori_loop(2, 34, window, 0)
-
-    def run_chunk(c):
-        base = c * CHUNK
+    lax.fori_loop(CHUNK // 8, CHUNK // 8 + 4, window, 0)
+
+    def run_chunk(base, size):
         lhs = jnp.concatenate(
             [
-                shifted[piece, pl.ds(base + 6 + 2 * m, CHUNK + 1)].reshape((CHUNK + 1) * 16, TB)
+                shifted[piece, pl.ds(base + 6 + 2 * m, size + 1)].reshape((size + 1) * 16, TB)
                 for m in range(11)
                 for piece in range(3)
             ],
             axis=1,
         )
         both = jnp.dot(lhs, band[...], preferred_element_type=F32)
-        sums[...] = both[:ROWS, :TB] + both[16:, TB:]
+        sums[0 : size * 16] = both[: size * 16, :TB] + both[16:, TB:]
+        tile = base // 32
         for j in range(N):
-            for b in range(CHUNK // 16):
-                sig[j, c * 2 + b // 2, (b % 2) * 16 : (b % 2) * 16 + 16, :] = sums[pl.ds(b * 256 + j, 16, stride=16), :].astype(BF16)
-
+            for b in range(size // 16):
+                sig[j, tile + b // 2, (b % 2) * 16 : (b % 2) * 16 + 16, :] = sums[
+                    pl.ds(b * 256 + j, 16, stride=16), :
+                ].astype(BF16)
         exchange(
             begin,
-            lambda j: sig.at[j, pl.ds(c * 2, 2)],
-            lambda h, i: recv[h].at[pl.ds(i * 8 + c * 2, 2)],
+            lambda j: sig.at[j, pl.ds(tile, size // 32)],
+            lambda h, i: recv[h].at[pl.ds(i * 8 + tile, size // 32)],
             tile_send,
             tile_recv,
         )
 
-    def middle(i, carry):
-        run_chunk(i + 1)
-        return carry
-
-    lax.fori_loop(0, 2, middle, 0)
-
-    for i in range(2, 8):
-        take_halo(i)
-    for side, base in ((0, 0), (1, 272 * 18)):
-        for j in range(N):
-            tall[pl.ds(base + j + 1, 16, stride=18), :] = halo_w[side, :, j * TB : (j + 1) * TB].astype(F32)
-        for t, j in ((0, 0), (1, 17)):
-            tall[pl.ds(base + j, 16, stride=18), :] = halo_c[side * 2 + t].astype(F32)
-    lax.fori_loop(0, 2, window, 0)
-    lax.fori_loop(34, 36, window, 0)
-
-    def outer(i, carry):
-        run_chunk(i * 3)
-        return carry
-
-    lax.fori_loop(0, 2, outer, 0)
+    own_refs = (lambda j: own_out.at[j], lambda h, i: own_in.at[h, i], own_send, own_recv)
+
+    def share_owners():
+        row = lax.broadcasted_iota(jnp.int32, (TB, TB), 0)
+        hit = jnp.where(roi_ref[0:1, :] == lax.rem(row, 8) * 16 + row // 8, roi_ref[1:2, :] + 1, 0)
+        table = jnp.dot(hit.astype(F32).astype(BF16), jnp.ones((TB, TB), BF16), preferred_element_type=F32)
+        own_out[...] = table.reshape(N, 8, TB)
+
+        exchange(begin, *own_refs)
+
+        @pl.when(whole)
+        def _():
+            own_in[0, spot] = own_out[mine]
+
+        @pl.when(split)
+        def _():
+            for h in range(2):
+                own_in[h, spot] = own_out[8 + 2 * plane + h]
+
+    def take_wires():
+        for i in range(2, 8):
+            take_halo(i)
+        for side, base in ((0, 0), (1, 272 * 18)):
+            for j in range(N):
+                tall[pl.ds(base + j + 1, 16, stride=18), :] = halo_w[side, :, j * TB : (j + 1) * TB].astype(F32)
+            for t, j in ((0, 0), (1, 17)):
+                tall[pl.ds(base + j, 16, stride=18), :] = halo_c[side * 2 + t].astype(F32)
+
+    chunks = 256 // CHUNK
+
+    def step(n, carry):
+        c = lax.rem(n + 1, chunks)
+        pl.when(n == chunks - 2)(take_wires)
+        slots = jnp.where(c == 0, 0, (c * CHUNK + 32) // 8)
+        lax.fori_loop(slots, slots + CHUNK // 8, window, 0)
+        run_chunk(c * CHUNK, CHUNK)
+        pl.when(n == 0)(share_owners)
+        return carry
+
+    lax.fori_loop(0, chunks, step, 0)
 
     def store_signal(j, carry):
         pltpu.make_async_copy(
@@ -467,7 +470,11 @@
         lax.fori_loop(0, BLOCKS, block, jnp.zeros((TB, TB), F32), unroll=UNROLL)
 
         for i in range(N):
-            o = lax.rem(me + 1 + i, N)
+            o = lax.rem(plane + 1 + i // 2, 4) * 4
+            if i < 8:
+                o += 2 * (1 - half) + i % 2
+            else:
+                o += 2 * half + lax.rem(inner + 1 + i, 2)
 
             def send_piece():
                 now = runs[h, jnp.clip(plan[h, 3, o], 0, BLOCKS)]
@@ -606,7 +613,7 @@
             pltpu.VMEM((TB, 2048), F32),
             pltpu.SemaphoreType.DMA((6, 4)),
         ],
-        compiler_params=pltpu.CompilerParams(vmem_limit_bytes=8 << 20),
+        compiler_params=pltpu.CompilerParams(vmem_limit_bytes=LIMIT),
         name="finish",
     )(signal, pieces)
 

time: 55.4 us -> 53 us (0.957)
  local copies, waits for them, and re-layouts: 2.35 us -> 0 us
    unnamed x4 -> x0, local copies, waits for them, and re-layouts: 2.35 us -> none
where the time goes in v5:
time: 53 us; the launch traced here: 52.7 us
  Pallas kernels  52.1 us (98%)
  between operations  0.64 us (1%)
    pallas_call x1, Pallas kernels, fused(): pl.pallas_call(kernel, out_shape=(jax.ShapeDtypeStruct((8, 32, 2048), BF1...  49.6 us
    pallas_call x1, Pallas kernels, finish(): pl.pallas_call(finish_kernel, out_shape=(jax.ShapeDtypeStruct((8, 32, 204...  2.49 us

profile of v5, /device:TPU:25, one launch (start us, length us, event | category | flops | bytes accessed | tf_op | source)
XLA Modules:
  0.0 52.7 jit_solution(9718495383978422172)
XLA Ops:
  0.6 49.6 %fused.1 = (bf16[8,32,2048]{2,1,0:T(8,128)(2,1)}, bf16[24,128,128]{2,1,0:T(8,128)(2,1)}) custom-call(bf16[256,2048]{1,0:T(8,128)(2,1)} %raw_hbm.1, s32[1,256]{1,0:T(1,128)} %bitcast.6, bf16[21,256]{1,0:T(8,128)(2,1)} %bitcast.5, s32[1,102]{1,0:T(1,128)} %bitcast.7, s32[1,102]{1,0:T(1,128)} %bitcast.8, bf16[128,32,128]{2,1,0:T(8,128)(2,1)} %geo_ref.1), custom_call_target="tpu_custom_call" | custom-call | tf_op jit(solution)/shard_map/fused/pallas_call | solution.py:623
  50.3 2.5 %finish.1 = (bf16[8,32,2048]{2,1,0:T(8,128)(2,1)}, f32[128,2048]{1,0:T(8,128)}) custom-call(bf16[8,32,2048]{2,1,0:T(8,128)(2,1)} %get-tuple-element.6.signal_ref, bf16[24,128,128]{2,1,0:T(8,128)(2,1)} %get-tuple-element.7.piece_ref), custom_call_target="tpu_custom_call" | custom-call | tf_op jit(solution)/shard_map/finish/pallas_call | solution.py:602

commit v6 on v5

--- a/solution.py
+++ b/solution.py
@@ -9,6 +9,7 @@
 N = 16
 CHUNK = 64
 ROWS = CHUNK * 16
+EARLY = 4
 BLOCKS = 22
 UNROLL = BLOCKS
 LIMIT = 56 << 20
@@ -24,7 +25,7 @@
     return ref.at[pl.ds(pl.multiple_of(index, size), size)]
 
 
-def build_bands(taps_ref, band_ref):
+def build_bands(taps_ref, band_ref, first, last):
     row = lax.broadcasted_iota(jnp.int32, (TB, TB), 0)
     col = lax.broadcasted_iota(jnp.int32, (TB, TB), 1)
     upper = col >= row
@@ -53,7 +54,7 @@
                 band_ref[pl.ds(start, TB), p * TB : (p + 1) * TB] = pieces[piece].astype(BF16)
         return carry
 
-    lax.fori_loop(0, 11, pair, 0)
+    lax.fori_loop(first, last, pair, 0)
 
 
 def kernel(
@@ -113,6 +114,8 @@
     def member(m):
         return (m // 4, lax.rem(m, 4), tick)
 
+    raw_copy = pltpu.make_async_copy(raw_hbm, raw_ref, local.at[3])
+    raw_copy.start()
     barrier = pltpu.get_barrier_semaphore()
 
     def greet(r, carry):
@@ -137,8 +140,6 @@
             when_all((t_key, *w_keys), greet_side)
     lax.fori_loop(1, N, greet, 0)
 
-    raw_copy = pltpu.make_async_copy(raw_hbm, raw_ref, local.at[3])
-    raw_copy.start()
     geo_copy = pltpu.make_async_copy(geo_ref, geo, local.at[0])
     taps[...] = jnp.zeros((24, 2 * TB), F32)
     taps[0:21, :] = taps_ref[...].astype(F32)
@@ -151,6 +152,7 @@
     diag = jnp.where(row == col, mask_ref[...].astype(F32), 0.0).astype(BF16)
     mask_col[...] = jnp.dot(diag, jnp.ones((256, TB), BF16), preferred_element_type=F32)
 
+    build_bands(taps, band, 0, EARLY)
     raw_copy.wait()
     geo_copy.start()
     for side, start in ((0, 0), (1, 15 * TB)):
@@ -281,7 +283,7 @@
             def _():
                 arrival(h, spot, dst, receive).wait_recv()
 
-    build_bands(taps, band)
+    build_bands(taps, band, EARLY, 11)
 
     def spread(i, carry):
         wires = pl.ds(pl.multiple_of(i * 16, 16), 16)

time: 53 us -> 53 us (level)
  no operation moved by 1% of the time
where the time goes in v6:
time: 53 us; the launch traced here: 52.7 us
  Pallas kernels  52.1 us (98%)
  between operations  0.64 us (1%)
    pallas_call x1, Pallas kernels, fused(): pl.pallas_call(kernel, out_shape=(jax.ShapeDtypeStruct((8, 32, 2048), BF1...  49.6 us
    pallas_call x1, Pallas kernels, finish(): pl.pallas_call(finish_kernel, out_shape=(jax.ShapeDtypeStruct((8, 32, 204...  2.49 us

profile of v6, /device:TPU:25, one launch (start us, length us, event | category | flops | bytes accessed | tf_op | source)
XLA Modules:
  0.0 52.7 jit_solution(12217563101230836578)
XLA Ops:
  0.6 49.6 %fused.1 = (bf16[8,32,2048]{2,1,0:T(8,128)(2,1)}, bf16[24,128,128]{2,1,0:T(8,128)(2,1)}) custom-call(bf16[256,2048]{1,0:T(8,128)(2,1)} %raw_hbm.1, s32[1,256]{1,0:T(1,128)} %bitcast.6, bf16[21,256]{1,0:T(8,128)(2,1)} %bitcast.5, s32[1,102]{1,0:T(1,128)} %bitcast.7, s32[1,102]{1,0:T(1,128)} %bitcast.8, bf16[128,32,128]{2,1,0:T(8,128)(2,1)} %geo_ref.1), custom_call_target="tpu_custom_call" | custom-call | tf_op jit(solution)/shard_map/fused/pallas_call | solution.py:625
  50.3 2.5 %finish.1 = (bf16[8,32,2048]{2,1,0:T(8,128)(2,1)}, f32[128,2048]{1,0:T(8,128)}) custom-call(bf16[8,32,2048]{2,1,0:T(8,128)(2,1)} %get-tuple-element.6.signal_ref, bf16[24,128,128]{2,1,0:T(8,128)(2,1)} %get-tuple-element.7.piece_ref), custom_call_target="tpu_custom_call" | custom-call | tf_op jit(solution)/shard_map/finish/pallas_call | solution.py:604

commit v7 on v6

--- a/solution.py
+++ b/solution.py
@@ -640,10 +640,10 @@
             pltpu.VMEM((2, 16, 2048), BF16),
             pltpu.VMEM((4, 16, TB), BF16),
             pltpu.VMEM((256, TB), F32),
-            pltpu.VMEM((288 * 18, TB), F32),
+            pltpu.VMEM((290 * 18 + 12, TB), F32),
             pltpu.VMEM((3, 288, 16, TB), BF16),
             pltpu.VMEM((33 * TB, 2 * TB), BF16),
-            pltpu.VMEM((ROWS, TB), F32),
+            pltpu.VMEM((ROWS + 32, TB), F32),
             pltpu.VMEM((N, 8, 32, TB), BF16),
             pltpu.VMEM((65, 32, TB), BF16),
             pltpu.VMEM((65, 32, TB), BF16),

time: 53 us -> 53.1 us (level)
  no operation moved by 1% of the time
where the time goes in v7:
time: 53.1 us; the launch traced here: 52.8 us
  Pallas kernels  52.1 us (98%)
  between operations  0.64 us (1%)
    pallas_call x1, Pallas kernels, fused(): pl.pallas_call(kernel, out_shape=(jax.ShapeDtypeStruct((8, 32, 2048), BF1...  49.6 us
    pallas_call x1, Pallas kernels, finish(): pl.pallas_call(finish_kernel, out_shape=(jax.ShapeDtypeStruct((8, 32, 204...  2.49 us

profile of v7, /device:TPU:25, one launch (start us, length us, event | category | flops | bytes accessed | tf_op | source)
XLA Modules:
  0.0 52.8 jit_solution(2658901771449537509)
XLA Ops:
  0.6 49.6 %fused.1 = (bf16[8,32,2048]{2,1,0:T(8,128)(2,1)}, bf16[24,128,128]{2,1,0:T(8,128)(2,1)}) custom-call(bf16[256,2048]{1,0:T(8,128)(2,1)} %raw_hbm.1, s32[1,256]{1,0:T(1,128)} %bitcast.6, bf16[21,256]{1,0:T(8,128)(2,1)} %bitcast.5, s32[1,102]{1,0:T(1,128)} %bitcast.7, s32[1,102]{1,0:T(1,128)} %bitcast.8, bf16[128,32,128]{2,1,0:T(8,128)(2,1)} %geo_ref.1), custom_call_target="tpu_custom_call" | custom-call | tf_op jit(solution)/shard_map/fused/pallas_call | solution.py:625
  50.3 2.5 %finish.1 = (bf16[8,32,2048]{2,1,0:T(8,128)(2,1)}, f32[128,2048]{1,0:T(8,128)}) custom-call(bf16[8,32,2048]{2,1,0:T(8,128)(2,1)} %get-tuple-element.6.signal_ref, bf16[24,128,128]{2,1,0:T(8,128)(2,1)} %get-tuple-element.7.piece_ref), custom_call_target="tpu_custom_call" | custom-call | tf_op jit(solution)/shard_map/finish/pallas_call | solution.py:604

commit v8 on v5

--- a/solution.py
+++ b/solution.py
@@ -578,9 +578,12 @@
                 pltpu.make_async_copy(held.at[span], signal_out.at[span], sem.at[5, g]),
             )
         )
-    for load in loads:
-        for copy in load:
-            copy.start()
+    for i in (2, 0, 1):
+        for load in loads:
+            load[i].start()
+    for g in range(4):
+        loads[g][2].wait()
+        stores[g][2].start()
     for g in range(4):
         loads[g][0].wait()
         loads[g][1].wait()
@@ -591,8 +594,6 @@
             ].astype(F32)
         stores[g][0].start()
         stores[g][1].start()
-        loads[g][2].wait()
-        stores[g][2].start()
     for store in stores:
         for copy in store:
             copy.wait()
@@ -638,10 +639,10 @@
             pltpu.VMEM((2, 16, 2048), BF16),
             pltpu.VMEM((4, 16, TB), BF16),
             pltpu.VMEM((256, TB), F32),
-            pltpu.VMEM((288 * 18, TB), F32),
+            pltpu.VMEM((290 * 18 + 12, TB), F32),
             pltpu.VMEM((3, 288, 16, TB), BF16),
             pltpu.VMEM((33 * TB, 2 * TB), BF16),
-            pltpu.VMEM((ROWS, TB), F32),
+            pltpu.VMEM((ROWS + 32, TB), F32),
             pltpu.VMEM((N, 8, 32, TB), BF16),
             pltpu.VMEM((65, 32, TB), BF16),
             pltpu.VMEM((65, 32, TB), BF16),

time: 53 us -> 53 us (level)
  no operation moved by 1% of the time
where the time goes in v8:
time: 53 us; the launch traced here: 52.8 us
  Pallas kernels  52.1 us (98%)
  between operations  0.64 us (1%)
    pallas_call x1, Pallas kernels, fused(): pl.pallas_call(kernel, out_shape=(jax.ShapeDtypeStruct((8, 32, 2048), BF1...  49.6 us
    pallas_call x1, Pallas kernels, finish(): pl.pallas_call(finish_kernel, out_shape=(jax.ShapeDtypeStruct((8, 32, 204...  2.5 us

profile of v8, /device:TPU:25, one launch (start us, length us, event | category | flops | bytes accessed | tf_op | source)
XLA Modules:
  0.0 52.8 jit_solution(16085961124340053149)
XLA Ops:
  0.6 49.6 %fused.1 = (bf16[8,32,2048]{2,1,0:T(8,128)(2,1)}, bf16[24,128,128]{2,1,0:T(8,128)(2,1)}) custom-call(bf16[256,2048]{1,0:T(8,128)(2,1)} %raw_hbm.1, s32[1,256]{1,0:T(1,128)} %bitcast.6, bf16[21,256]{1,0:T(8,128)(2,1)} %bitcast.5, s32[1,102]{1,0:T(1,128)} %bitcast.7, s32[1,102]{1,0:T(1,128)} %bitcast.8, bf16[128,32,128]{2,1,0:T(8,128)(2,1)} %geo_ref.1), custom_call_target="tpu_custom_call" | custom-call | tf_op jit(solution)/shard_map/fused/pallas_call | solution.py:624
  50.3 2.5 %finish.1 = (bf16[8,32,2048]{2,1,0:T(8,128)(2,1)}, f32[128,2048]{1,0:T(8,128)}) custom-call(bf16[8,32,2048]{2,1,0:T(8,128)(2,1)} %get-tuple-element.6.signal_ref, bf16[24,128,128]{2,1,0:T(8,128)(2,1)} %get-tuple-element.7.piece_ref), custom_call_target="tpu_custom_call" | custom-call | tf_op jit(solution)/shard_map/finish/pallas_call | solution.py:603
